TPU v7x, 512 devices: a whole 4x4x16 slice. The times are simulated.
512 devices in a mesh: seq: 64 (over y_lo, z, core), kv: 8 (over x, y_hi).
Axes of the slice: x: 4, y: 4 (y_hi: 2, y_lo: 2; y = y_hi * 2 + y_lo), z: 16, core: 2. Of those that a mesh axis runs over, the one named last changes fastest.
Arguments:
- queries: bfloat16 [64, 16384, 128], P('kv', 'seq'), may hold values from -56 to 56
- key_states: bfloat16 [8, 16384, 128], P('kv', 'seq'), may hold values from -56 to 56
- samples: int32 [64, 512], P('kv', 'seq'), may hold values from 0 to 16383, as said below
- query_gate_weight: float32 [128, 128], replicated, may hold values from -6 to 6
- key_gate_weight: float32 [384, 128], replicated, may hold values from -0.3125 to 0.3125
Outputs:
- row_loss: float32 [64, 512], P('kv', 'seq')
- query_grad: float32 [128, 128], replicated
- key_grad: float32 [384, 128], replicated
Inputs may be any that keep to these rules, and one draw needn't show every extreme that they name: `samples`: sampled row r of every head lies in the tokens r // 8 * 256 to (r // 8 + 1) * 256 - 1; positions may repeat.
All inputs are finite; a program needn't handle non-finite values.
Results may differ from a plain program's by a relative error of at most 0.0003.
Values may be sent and summed in bfloat16 or wider, within the bound.
A program may use at most 64 MiB of HBM per device.

v0:
```python
import math

import jax
import jax.numpy as jnp
from jax import lax
from jax.sharding import Mesh
from jax.sharding import PartitionSpec as P

BLOCK = 128
SEQ = ("seq_0", "seq_1", "seq_2")
SEQ_KV = ("seq_0", "seq_1", "seq_2", "kv")


masked_score = -1e30
highest = lax.Precision.HIGHEST


def laid_out(tiles, dim):
    shape = list(tiles.shape[1:])
    shape[dim] *= tiles.shape[0]
    return jnp.moveaxis(tiles, 0, dim).reshape(shape)


def gather_in_order(array, axes, sequence):
    tiles = array[None]
    for k in sequence:
        tiles = lax.all_gather(tiles, axes[k], axis=0, tiled=True)
    held = [lax.axis_size(axes[k]) for k in reversed(sequence)]
    tiles = tiles.reshape(*held, *array.shape)
    turned = sorted(range(len(sequence)), key=lambda place: sequence[len(sequence) - 1 - place])
    return tiles.transpose(*turned, *range(len(sequence), tiles.ndim)).reshape(-1, *array.shape)


def gathered_by_axis(array, axes, sequence, dim):
    return laid_out(gather_in_order(array, axes, sequence), dim)


def from_everyone(array, axis):
    copies = jnp.broadcast_to(array, (lax.axis_size(axis), *array.shape))
    return lax.all_to_all(copies, axis, split_axis=0, concat_axis=0, tiled=True)


def gather_directly(array, axis, dim):
    return laid_out(from_everyone(array, axis), dim)


def in_blocks(array, dim, peers):
    shape = array.shape
    tiles = array.reshape(*shape[:dim], peers, shape[dim] // peers, *shape[dim + 1 :])
    return jnp.moveaxis(tiles, dim, 0)


def sent_and_summed(array, axis, dim):
    tiles = in_blocks(array, dim, lax.axis_size(axis))
    arrived = lax.all_to_all(tiles, axis, split_axis=0, concat_axis=0, tiled=True)
    return arrived.sum(axis=0)


def in_one(arrays, axis):
    ends = [0]
    for a in arrays:
        ends.append(ends[-1] + a.size)
    so_far = lax.psum(jnp.concatenate([a.ravel() for a in arrays]), axis)
    return tuple((so_far[b:e].reshape(a.shape) for a, b, e in zip(arrays, ends, ends[1:])))


def score_tile(row_block, key_block):
    return lax.dot_general(
        row_block, key_block, (((1,), (1,)), ((), ())), preferred_element_type=jnp.float32
    )


def body(queries, key_states, samples, query_gate_weight, key_gate_weight):
    head_count, shard_len, head_width = queries.shape
    rows_local = samples.shape[1]
    gate_width = query_gate_weight.shape[1]
    seq_devices = lax.axis_size(SEQ)
    shard_index = lax.axis_index(SEQ)
    offset = shard_index * shard_len
    local_blocks = shard_len // BLOCK
    total_blocks = local_blocks * seq_devices
    score_scale = 1.0 / math.sqrt(head_width)
    gate_scale = 1.0 / math.sqrt(gate_width)
    pooled_query = jnp.mean(
        queries.reshape(head_count, local_blocks, BLOCK, head_width), axis=2, dtype=jnp.float32
    )
    key_rows = key_states[0]
    key_blocks = key_rows.reshape(local_blocks, BLOCK, head_width)
    pooled_key = jnp.concatenate(
        [
            jnp.max(key_blocks, axis=1).astype(jnp.float32),
            jnp.min(key_blocks, axis=1).astype(jnp.float32),
            jnp.mean(key_blocks, axis=1, dtype=jnp.float32),
        ],
        axis=-1,
    )
    gate_key = jnp.dot(pooled_key, key_gate_weight, precision=highest)
    local_places = samples - offset
    query_rows = jnp.take_along_axis(queries, local_places[:, :, None], axis=1)
    row_count = head_count * rows_local
    flat_rows = query_rows.reshape(row_count, head_width)
    flat_places = samples.reshape(row_count)
    initial = (
        jnp.full((row_count,), masked_score, jnp.float32),
        jnp.zeros((row_count, total_blocks), jnp.float32),
    )
    pieces = gathered_by_axis(key_rows, SEQ, (0, 1, 2), 0).reshape(-1, shard_len, head_width)

    def absorb_one(turn_number, running):
        running_top, running_mass = running
        first_key = turn_number * shard_len
        scores = score_tile(flat_rows, pieces[turn_number]) * score_scale
        causal = (first_key + jnp.arange(shard_len, dtype=jnp.int32))[None, :] <= flat_places[
            :, None
        ]
        tile_top = jnp.max(jnp.where(causal, scores, masked_score), axis=1)
        new_top = jnp.maximum(running_top, tile_top)
        weights = jnp.where(causal, jnp.exp(scores - new_top[:, None]), 0.0)
        tile_mass = jnp.sum(weights.reshape(row_count, local_blocks, BLOCK), axis=2)
        rescaled = running_mass * jnp.exp(running_top - new_top)[:, None]
        placed = lax.dynamic_update_slice(rescaled, tile_mass, (jnp.int32(0), first_key // BLOCK))
        return (new_top, placed)

    running_top, running_mass = lax.fori_loop(0, pieces.shape[0], absorb_one, initial)
    teacher = running_mass / jnp.sum(running_mass, axis=1, keepdims=True)
    every_key = gather_directly(gate_key, SEQ, 0)
    gate_query = jnp.einsum("hcd,dg->hcg", pooled_query, query_gate_weight, precision=highest)
    local_block = local_places // BLOCK
    gate_rows = jnp.take_along_axis(gate_query, local_block[:, :, None], axis=1).reshape(
        row_count, gate_width
    )
    pooled_rows = jnp.take_along_axis(pooled_query, local_block[:, :, None], axis=1).reshape(
        row_count, head_width
    )
    own_block = flat_places // BLOCK
    allowed = jnp.arange(total_blocks, dtype=jnp.int32)[None, :] <= own_block[:, None]
    logits = jnp.dot(gate_rows, every_key.T, precision=highest) * gate_scale
    logit_top = jnp.max(jnp.where(allowed, logits, masked_score), axis=1)
    gate_weights = jnp.where(allowed, jnp.exp(logits - logit_top[:, None]), 0.0)
    gate_total = jnp.sum(gate_weights, axis=1)
    log_total = logit_top + jnp.log(gate_total)
    flat_loss = log_total - jnp.sum(jnp.where(allowed, teacher * logits, 0.0), axis=1)
    gate_delta = jnp.where(allowed, gate_weights / gate_total[:, None] - teacher, 0.0)
    query_part = jnp.dot(
        pooled_rows.T,
        jnp.dot(gate_delta, every_key, precision=highest) * gate_scale,
        precision=highest,
    )
    key_delta = sent_and_summed(
        jnp.dot(gate_delta.T, gate_rows, precision=highest) * gate_scale, SEQ, 0
    )
    key_part = jnp.dot(pooled_key.T, key_delta, precision=highest)
    row_loss = flat_loss.reshape(head_count, rows_local)
    query_grad, key_grad = in_one((query_part, key_part), SEQ_KV)
    return (row_loss, query_grad, key_grad)


def solution(mesh):
    torus = Mesh(
        mesh.devices.reshape(2, 16, 2, mesh.shape["kv"]), ("seq_0", "seq_1", "seq_2", "kv")
    )
    placed = (P("kv", SEQ, None), P("kv", SEQ, None), P("kv", SEQ), P(), P())
    return jax.shard_map(
        body, mesh=torus, in_specs=placed, out_specs=(P("kv", SEQ), P(), P()), check_vma=False
    )
```

profile of v0, /device:TPU:1, one launch (start us, length us, event | category | flops | bytes accessed | tf_op | source)
XLA Modules:
  0.0 740.9 jit_solution(1190638927435643087)
XLA Ops:
  7.2 6.3 all_gather.9
  13.6 68.6 %all-gather.3.cloned.1.call-done = bf16[32,256,128]{2,1,0:T(8,128)(2,1)} async-done(((bf16[2,256,128]{2,1,0:T(8,128)(2,1)}), bf16[32,256,128]{2,1,0:T(8,128)(2,1)}) %all-gather.3.cloned.1.call-update) | async-done | bytes 2097168 | tf_op jit(solution)/shard_map/all_gather | solution.py:27
  84.9 19.1 %all-to-all-start = ((f32[64,2,128]{2,1,0:T(2,128)}), f32[64,2,128]{2,1,0:T(2,128)S(1)}, u32[]{:S(2)}, u32[]{:S(2)}) async-start(f32[64,2,128]{2,1,0:T(2,128)} %broadcast_in_dim.73), calls=%async_computation | async-start | bytes 131072 | tf_op jit(solution)/shard_map/all_to_all | solution.py:40
  104.8 1.1 convert_reduce_fusion
  111.6 1.7 gather_fusion
  113.4 5.1 all-to-all-done
  119.0 4.7 copy.13
  123.6 125.2 %while.19 = (s32[]{:T(128)}, f32[64]{0:T(128)S(1)}, f32[64,128]{1,0:T(8,128)S(1)}, s32[8,8]{1,0:T(8,128)}, bf16[64,256,128]{2,1,0:T(8,128)(2,1)}, /*index=5*/bf1...) while((s32[]{:T(128)}, f32[64]{0:T(128)S(1)}, ...), condition=%wide.wide.region_9.11_spmd.clone, body=%wide.wide.region_6.10_spmd.clone.sunk | while | flops 4333846 | bytes 548455 | solution.py:124
  133.3 1.1 fusion.39
  139.1 1.1 fusion.39
  145.0 1.1 fusion.39
  154.8 1.1 fusion.39
  160.7 1.1 fusion.39
  170.5 1.1 fusion.39
  176.4 1.1 fusion.39
  182.2 1.1 fusion.39
  192.0 1.1 fusion.39
  197.9 1.1 fusion.39
  207.7 1.1 fusion.39
  250.1 9.9 %all-to-all-start.1 = ((f32[64,2,128]{2,1,0:T(2,128)}), f32[64,2,128]{2,1,0:T(2,128)S(1)}, u32[]{:S(2)}, u32[]{:S(2)}) async-start(f32[64,2,128]{2,1,0:T(2,128)} %bitcast.16), calls=%async_computation.1 | async-start | bytes 131072 | tf_op jit(solution)/shard_map/all_to_all | solution.py:55
  260.8 13.9 %all-to-all-done.1 = f32[64,2,128]{2,1,0:T(2,128)S(1)} async-done(((f32[64,2,128]{2,1,0:T(2,128)}), f32[64,2,128]{2,1,0:T(2,128)S(1)}, u32[]{:S(2)}, u32[]{:S(2)}) %all-to-all-start.1) | async-done | bytes 65568 | tf_op jit(solution)/shard_map/all_to_all | solution.py:55
  276.7 454.6 %all-reduce.2.cloned.1.call-done = f32[65536]{0:T(1024)} async-done(((f32[65536]{0:T(1024)}), f32[65536]{0:T(1024)}) %all-reduce.2.cloned.1.call-update) | async-done | bytes 262160 | tf_op jit(solution)/shard_map/psum | solution.py:63
  731.3 1.6 slice_bitcast_fusion
  732.9 1.5 slice_bitcast_fusion.1
  (545 shorter events, 120.9 us)
Async XLA Ops:
  7.2 76.8 %copy-start = (f32[384,128]{1,0:T(8,128)S(1)}, f32[384,128]{1,0:T(8,128)}, u32[]{:S(2)}) copy-start(f32[384,128]{1,0:T(8,128)} %param.13) | copy-start | bytes 589828
  7.2 75.0 %all-gather.3.cloned.1.call-start = ((), (), s32[]{:S(2)}) async-start(), calls=%async_computation.2 | async-start | bytes 2228224 | tf_op jit(solution)/shard_map/all_gather | solution.py:27
  13.6 105.4 %all-gather.5.cloned.1.call-start = ((), (), s32[]{:S(2)}) async-start(), calls=%async_computation.3 | async-start | bytes 6291456 | tf_op jit(solution)/shard_map/all_gather | solution.py:27
  84.9 33.7 %all-to-all-start = ((f32[64,2,128]{2,1,0:T(2,128)}), f32[64,2,128]{2,1,0:T(2,128)S(1)}, u32[]{:S(2)}, u32[]{:S(2)}) async-start(f32[64,2,128]{2,1,0:T(2,128)} %broadcast_in_dim.73), calls=%async_computation | async-start | bytes 131072 | tf_op jit(solution)/shard_map/all_to_all | solution.py:40
  250.1 24.5 %all-to-all-start.1 = ((f32[64,2,128]{2,1,0:T(2,128)}), f32[64,2,128]{2,1,0:T(2,128)S(1)}, u32[]{:S(2)}, u32[]{:S(2)}) async-start(f32[64,2,128]{2,1,0:T(2,128)} %bitcast.16), calls=%async_computation.1 | async-start | bytes 131072 | tf_op jit(solution)/shard_map/all_to_all | solution.py:55
  260.1 471.2 %all-reduce.2.cloned.1.call-start = ((), (), s32[]{:S(2)}) async-start(), calls=%async_computation.4 | async-start | bytes 524288 | tf_op jit(solution)/shard_map/psum | solution.py:63
Sparse Core Ops, SparseCore 0:
  13.7 68.4 all-gather.2
  84.3 31.6 all-gather.4
  276.1 455.1 all-reduce.1
where the time goes:
time: 745 us; the launch traced here: 741 us
  waiting for transfers between devices  542 us (73%)
  matrix products  74.3 us (10%)
  local copies, waits for them, and re-layouts  42.7 us (6%)
  starting transfers between devices  29.2 us (4%)
  other arithmetic  26.4 us (4%)
  between operations  13.9 us (2%)
    psum x1, waiting for transfers between devices, in_one(): so_far = lax.psum(jnp.concatenate([a.ravel() for a in arrays]), axis)  455 us
    dot_general x64, matrix products, score_tile(): lax.dot_general(row_block, key_block, (((1,), (1,)), ((), ())), preferred...  70.5 us
    all_gather x2, waiting for transfers between devices, gather_in_order(): tiles = lax.all_gather(tiles, axes[k], axis=0, tiled=True)  68.6 us
    dynamic_update_slice x64, local copies, waits for them, and re-layouts, absorb_one(): lax.dynamic_update_slice(rescaled, tile_mass, (jnp.int32(0), first_key //...  26.3 us
    all_to_all x1, starting transfers between devices, from_everyone(): return lax.all_to_all(copies, axis, split_axis=0, concat_axis=0, tiled=True)  19.1 us
  transfers between devices with their start and end apart: 5, of which 4 were waited for; matrix products, arithmetic and copies ran while one was open for 2% of the time, Pallas kernels for 0%

commit v1 on v0

v1 whole, which is shorter than its diff:
```python
import functools
import math

import jax
import jax.numpy as jnp
from jax import lax
from jax.experimental import pallas as pl
from jax.experimental.pallas import tpu as pltpu
from jax.sharding import Mesh
from jax.sharding import PartitionSpec as P

BLOCK = 128
PIECES = 4
MESH = pl.DeviceIdType.MESH
LOW = -1e30
highest = lax.Precision.HIGHEST
NN = (((1,), (0,)), ((), ()))
NT = (((1,), (1,)), ((), ()))
TN = (((0,), (0,)), ((), ()))


def dot32(a, b, dims=NN):
    return lax.dot_general(a, b, dims, precision=highest, preferred_element_type=jnp.float32)


def partner(place, apart, size):
    if apart == 0:
        return place
    if size == 2:
        return 1 - place
    return (place + 1 - 2 * (place % 2), (place + 2) % 4, 3 - place)[apart - 1]


def kernel(
    sizes,
    q_ref,
    k_ref,
    samples_ref,
    wq_ref,
    wk_ref,
    loss_ref,
    query_grad_ref,
    key_grad_ref,
    keys,
    pooled,
    queries,
    top,
    mass,
    packed,
    returned,
    part,
    from_core,
    chip_sum,
    from_x,
    x_sum,
    from_y,
    y_sum,
    from_z,
    z_sum,
    y_all,
    x_all,
    whole,
    key_send,
    key_recv,
    pool_send,
    pool_recv,
    slice_send,
    slice_recv,
    sum_send,
    sum_recv,
    z_send,
    z_recv,
):
    nz, nx, nyh = sizes
    ny = 2 * nyh
    half = nz // 2
    z, yl, c = lax.axis_index("z"), lax.axis_index("yl"), lax.axis_index("c")
    x, yh = lax.axis_index("x"), lax.axis_index("yh")
    y = 2 * yh + yl
    started = []

    def send(src, dst, send_sem, recv_sem, target):
        copy = pltpu.make_async_remote_copy(
            src_ref=src,
            dst_ref=dst,
            send_sem=send_sem,
            recv_sem=recv_sem,
            device_id=target,
            device_id_type=MESH,
        )
        copy.start()
        started.append(copy)
        return copy

    def along_z(step):
        return {"z": (z + step + nz) % nz}

    def in_slice(i):
        return {"yl": partner(yl, i // 2, 2), "c": partner(c, i % 2, 2)}

    def along_x(i):
        return {"x": partner(x, i, nx)}

    def along_y(i):
        other = partner(y, i, ny)
        return {"yh": other // 2, "yl": other % 2}

    near = [along_z(1)] + ([along_z(-1)] if nz > 2 else [])
    near += [in_slice(i) for i in (1, 2, 3)]
    near += [along_x(i) for i in range(1, nx)]
    near += [along_y(i) for i in range(2, ny)]
    barrier = pltpu.get_barrier_semaphore()
    for target in near:
        pl.semaphore_signal(barrier, inc=1, device_id=target, device_id_type=MESH)

    own = k_ref[0].astype(jnp.float32)
    blocks = (own[:BLOCK], own[BLOCK:])
    pooled[0, 0] = jnp.concatenate(
        [jnp.max(b, axis=0, keepdims=True) for b in blocks]
        + [jnp.min(b, axis=0, keepdims=True) for b in blocks]
        + [jnp.sum(b, axis=0, keepdims=True) * (1.0 / BLOCK) for b in blocks]
        + [jnp.zeros((2, own.shape[1]), jnp.float32)],
        axis=0,
    )

    pl.semaphore_wait(barrier, len(near))

    rows_piece = k_ref.shape[1] // PIECES
    ways = ((0, 1, half), (1, -1, nz - 1 - half))

    def slot(way, step):
        return step if way == 0 else (nz - step) % nz

    def pass_keys(way, step, piece):
        rows = pl.ds(piece * rows_piece, rows_piece)
        src = k_ref.at[0, rows] if step == 0 else keys.at[slot(way, step), rows]
        return send(
            src,
            keys.at[slot(way, step + 1), rows],
            key_send.at[way, step, piece],
            key_recv.at[way, step, piece],
            along_z(ways[way][1]),
        )

    def pass_pooled(way, step):
        return send(
            pooled.at[slot(way, step)],
            pooled.at[slot(way, step + 1)],
            pool_send.at[way, step],
            pool_recv.at[way, step],
            along_z(ways[way][1]),
        )

    key_copies, pool_copies = {}, {}
    for piece in range(PIECES):
        for way, _, reach in ways:
            if reach:
                key_copies[way, 0, piece] = pass_keys(way, 0, piece)
    pooled_here = [
        send(
            pooled.at[0, 0],
            pooled.at[0, i],
            slice_send.at[0, i - 1],
            slice_recv.at[0, i - 1],
            in_slice(i),
        )
        for i in (1, 2, 3)
    ]

    shard = (yl * nz + z) * 2 + c
    local = (samples_ref[...] - shard * (2 * BLOCK)).astype(jnp.float32)
    spread = jnp.concatenate([jnp.broadcast_to(local[h : h + 1], (8, 8)) for h in range(8)], axis=0)
    lanes8 = lax.broadcasted_iota(jnp.int32, (64, 8), 1)
    rows8 = lax.broadcasted_iota(jnp.int32, (64, 8), 0) % 8
    column = jnp.sum(jnp.where(lanes8 == rows8, spread, 0.0), axis=1, keepdims=True)
    tokens = lax.broadcasted_iota(jnp.int32, (8, 2 * BLOCK), 1)
    query_rows, pooled_rows = [], []
    for h in range(8):
        place = column[8 * h : 8 * h + 8].astype(jnp.int32)
        chosen = jnp.where(tokens == place, 1.0, 0.0)
        block = jnp.where(tokens // BLOCK == place // BLOCK, 1.0, 0.0)
        both = lax.dot_general(
            jnp.concatenate([chosen, block], axis=0).astype(jnp.bfloat16),
            q_ref[h],
            NN,
            preferred_element_type=jnp.float32,
        )
        query_rows.append(both[:8])
        pooled_rows.append(both[8:] * (1.0 / BLOCK))
    queries[0] = jnp.concatenate(query_rows, axis=0).astype(jnp.bfloat16)
    queries_here = [
        send(
            queries.at[0],
            queries.at[i],
            slice_send.at[1, i - 1],
            slice_recv.at[1, i - 1],
            in_slice(i),
        )
        for i in (1, 2, 3)
    ]
    pooled_rows = jnp.concatenate(pooled_rows + [jnp.zeros((64, BLOCK), jnp.float32)], axis=0)
    gate_rows = dot32(pooled_rows, wq_ref[...])
    lanes = lax.broadcasted_iota(jnp.int32, (1, 256), 1)
    eye = lax.broadcasted_iota(jnp.int32, (64, 256), 0) == lax.broadcasted_iota(
        jnp.int32, (64, 256), 1
    )
    places = jnp.sum(jnp.where(eye, column, 0.0), axis=0, keepdims=True).astype(jnp.int32)
    places = jnp.where(lanes < 64, places, 2 * BLOCK - 1)

    for copy in queries_here:
        copy.wait_recv()
    every_query = queries[...].reshape(256, BLOCK)
    exponent = math.log2(math.e) / math.sqrt(BLOCK)

    def score(place):
        block_keys = k_ref[0] if place == 0 else keys[place]
        scores = lax.dot_general(block_keys, every_query, NT, preferred_element_type=jnp.float32)
        if place == 0:
            token = lax.broadcasted_iota(jnp.int32, scores.shape, 0)
            scores = jnp.where(token <= places, scores, LOW)
        for b in range(2):
            part_scores = scores[b * BLOCK : (b + 1) * BLOCK]
            highest_score = jnp.max(part_scores, axis=0, keepdims=True)
            weights = jnp.exp2((part_scores - highest_score) * exponent)
            at = b * nz + place
            top[at : at + 1] = highest_score
            mass[at : at + 1] = jnp.sum(weights, axis=0, keepdims=True)

    score(0)
    for step in range(1, half + 1):
        for piece in range(PIECES):
            for way, _, reach in ways:
                if step <= reach:
                    key_copies[way, step - 1, piece].wait_recv()
                    if step < reach:
                        key_copies[way, step, piece] = pass_keys(way, step, piece)
        if step == 1:
            for copy in pooled_here:
                copy.wait_recv()
        for way, _, reach in ways:
            if 1 < step <= reach + 1:
                pool_copies[way, step - 2].wait_recv()
            if step <= reach:
                pool_copies[way, step - 1] = pass_pooled(way, step - 1)
        for way, _, reach in ways:
            if step <= reach:
                score(slot(way, step))

    first = lax.broadcasted_iota(jnp.int32, (2 * nz, BLOCK), 1) < 64
    for pair in range(2):
        tops = top[:, pair * BLOCK : (pair + 1) * BLOCK]
        masses = mass[:, pair * BLOCK : (pair + 1) * BLOCK]
        packed[2 * pair] = jnp.where(first, tops, pltpu.roll(masses, 64, 1))
        packed[2 * pair + 1] = jnp.where(first, pltpu.roll(tops, 64, 1), masses)
    returns = [
        send(
            packed.at[i],
            returned.at[i],
            slice_send.at[2, i - 1],
            slice_recv.at[2, i - 1],
            in_slice(i),
        )
        for i in (1, 2, 3)
    ]
    for way, _, reach in ways:
        if reach == half:
            pool_copies[way, reach - 1].wait_recv()

    nb = 8 * nz
    pooled_keys = jnp.concatenate(
        [
            jnp.concatenate(
                [
                    pooled[:, i, 2 * kind + b : 2 * kind + b + 1, :].reshape(nz, BLOCK)
                    for kind in range(3)
                ],
                axis=1,
            )
            for i in range(4)
            for b in range(2)
        ],
        axis=0,
    )
    gate_key = dot32(pooled_keys, wk_ref[...])
    gate_scale = 1.0 / math.sqrt(BLOCK)
    logits = dot32(gate_key, gate_rows, NT) * gate_scale
    order = lax.broadcasted_iota(jnp.int32, (nb, BLOCK), 0)
    lane = lax.broadcasted_iota(jnp.int32, (nb, BLOCK), 1)
    i_of = order // (2 * nz)
    b_of = order // nz % 2
    z_of = (z - order % nz + nz) % nz
    yl_of = (yl + i_of // 2) % 2
    c_of = (c + i_of % 2) % 2
    block_of = ((yl_of * nz + z_of) * 2 + c_of) * 2 + b_of
    own_block = 2 * shard + places[:, :BLOCK] // BLOCK
    allowed = block_of <= own_block
    logit_top = jnp.max(jnp.where(allowed, logits, LOW), axis=0, keepdims=True)
    gate_weights = jnp.where(allowed, jnp.exp(logits - logit_top), 0.0)
    gate_total = jnp.sum(gate_weights, axis=0, keepdims=True)
    log_total = logit_top + jnp.log(gate_total)
    gate = gate_weights / gate_total

    for copy in returns:
        copy.wait_recv()
    pairs = jnp.concatenate([packed[0]] + [returned[i] for i in (1, 2, 3)], axis=0)
    sums = pltpu.roll(pairs, 64, 1)
    row_top = jnp.max(jnp.where(allowed, pairs, LOW), axis=0, keepdims=True)
    masses = jnp.where(allowed, sums * jnp.exp2((pairs - row_top) * exponent), 0.0)
    teacher = masses / jnp.sum(masses, axis=0, keepdims=True)
    losses = log_total - jnp.sum(jnp.where(allowed, teacher * logits, 0.0), axis=0, keepdims=True)
    delta = jnp.where(allowed & (lane < 64), (gate - teacher) * gate_scale, 0.0)

    head_of = lax.broadcasted_iota(jnp.int32, (8, BLOCK), 1) // 8
    head = lax.broadcasted_iota(jnp.int32, (8, BLOCK), 0)
    row_of = lax.broadcasted_iota(jnp.int32, (BLOCK, BLOCK), 0) % 8
    row = lax.broadcasted_iota(jnp.int32, (BLOCK, BLOCK), 1)

    block_query = dot32(delta, pooled_rows)
    local_sum = dot32(block_query, pooled_keys, TN)
    part[0] = local_sum[:, :256]
    part[1, :, :BLOCK] = local_sum[:, 256:]
    part[1, :, BLOCK:] = jnp.zeros((BLOCK, BLOCK), jnp.float32)
    other_core = {"c": 1 - c}
    copy = send(part.at[1 - c], from_core, sum_send.at[0], sum_recv.at[0], other_core)
    by_head = jnp.where(head_of == head, jnp.broadcast_to(losses, (8, BLOCK)), 0.0)
    loss_ref[...] = dot32(by_head, jnp.where(row_of == row, 1.0, 0.0))[:, :8]
    copy.wait_recv()
    chip_sum[...] = part[c] + from_core[...]

    rows_x = BLOCK // nx
    copies = [
        send(
            chip_sum.at[pl.ds(pl.multiple_of(partner(x, i, nx) * rows_x, rows_x), rows_x)],
            from_x.at[i],
            sum_send.at[i],
            sum_recv.at[i],
            along_x(i),
        )
        for i in range(1, nx)
    ]
    total = chip_sum[pl.ds(pl.multiple_of(x * rows_x, rows_x), rows_x)]
    for i, copy in enumerate(copies):
        copy.wait_recv()
        total = total + from_x[i + 1]
    x_sum[...] = total

    rows_y = rows_x // ny
    copies = [
        send(
            x_sum.at[pl.ds(pl.multiple_of(partner(y, i, ny) * rows_y, rows_y), rows_y)],
            from_y.at[i],
            sum_send.at[3 + i],
            sum_recv.at[3 + i],
            along_y(i),
        )
        for i in range(1, ny)
    ]
    total = x_sum[pl.ds(pl.multiple_of(y * rows_y, rows_y), rows_y)]
    for i, copy in enumerate(copies):
        copy.wait_recv()
        total = total + from_y[i + 1]
    y_sum[...] = total

    far_first = sorted(range(1, nz), key=lambda d: -min(d, nz - d))
    copies = [
        send(y_sum, from_z.at[z], z_send.at[d - 1], z_recv.at[d - 1], along_z(d)) for d in far_first
    ]
    from_z[z] = total
    for copy in copies:
        copy.wait_recv()
    total = from_z[0]
    for i in range(1, nz):
        total = total + from_z[i]

    z_sum[...] = total
    here = pl.ds(pl.multiple_of(y * rows_y, rows_y), rows_y)
    copies = [
        send(z_sum, y_all.at[here], sum_send.at[6 + i], sum_recv.at[6 + i], along_y(i))
        for i in range(1, ny)
    ]
    y_all[here] = total
    for copy in copies:
        copy.wait_recv()
    here = pl.ds(pl.multiple_of(x * rows_x, rows_x), rows_x)
    copies = [
        send(y_all, x_all.at[here], sum_send.at[9 + i], sum_recv.at[9 + i], along_x(i))
        for i in range(1, nx)
    ]
    x_all[here] = y_all[...]
    for copy in copies:
        copy.wait_recv()
    copy = send(x_all, whole.at[c], sum_send.at[13], sum_recv.at[13], other_core)
    whole[c] = x_all[...]
    copy.wait_recv()
    total = jnp.concatenate([whole[0], whole[1, :, :BLOCK]], axis=1)
    query_grad_ref[...] = dot32(total, wk_ref[...])
    key_grad_ref[...] = dot32(total, wq_ref[...], TN)
    for copy in started:
        copy.wait_send()


def body(sizes, queries, key_states, samples, query_gate_weight, key_gate_weight):
    nz, nx, nyh = sizes
    ny = 2 * nyh
    rows_x = BLOCK // nx
    rows_y = rows_x // ny
    f32, bf16 = jnp.float32, jnp.bfloat16
    dma = pltpu.SemaphoreType.DMA
    vmem = pl.BlockSpec(memory_space=pltpu.VMEM)
    half = nz // 2
    return pl.pallas_call(
        functools.partial(kernel, sizes),
        out_shape=(
            jax.ShapeDtypeStruct((8, 8), f32),
            jax.ShapeDtypeStruct((BLOCK, BLOCK), f32),
            jax.ShapeDtypeStruct((3 * BLOCK, BLOCK), f32),
        ),
        in_specs=[vmem] * 5,
        out_specs=(vmem,) * 3,
        scratch_shapes=[
            pltpu.VMEM((nz, 2 * BLOCK, BLOCK), bf16),
            pltpu.VMEM((nz, 4, 8, BLOCK), f32),
            pltpu.VMEM((4, 64, BLOCK), bf16),
            pltpu.VMEM((2 * nz, 256), f32),
            pltpu.VMEM((2 * nz, 256), f32),
            pltpu.VMEM((4, 2 * nz, BLOCK), f32),
            pltpu.VMEM((4, 2 * nz, BLOCK), f32),
            pltpu.VMEM((2, BLOCK, 256), f32),
            pltpu.VMEM((BLOCK, 256), f32),
            pltpu.VMEM((BLOCK, 256), f32),
            pltpu.VMEM((4, rows_x, 256), f32),
            pltpu.VMEM((rows_x, 256), f32),
            pltpu.VMEM((4, rows_y, 256), f32),
            pltpu.VMEM((rows_y, 256), f32),
            pltpu.VMEM((nz, rows_y, 256), f32),
            pltpu.VMEM((rows_y, 256), f32),
            pltpu.VMEM((rows_x, 256), f32),
            pltpu.VMEM((BLOCK, 256), f32),
            pltpu.VMEM((2, BLOCK, 256), f32),
            dma((2, half, PIECES)),
            dma((2, half, PIECES)),
            dma((2, half)),
            dma((2, half)),
            dma((3, 3)),
            dma((3, 3)),
            dma((14,)),
            dma((14,)),
            dma((nz,)),
            dma((nz,)),
        ],
        compiler_params=pltpu.CompilerParams(collective_id=0, has_side_effects=True),
    )(queries, key_states, samples, query_gate_weight, key_gate_weight)


SEQ = ("yl", "z", "c")
KV = ("x", "yh")


def build(mesh, sizes):
    nz, nx, nyh = sizes
    torus = Mesh(mesh.devices.reshape(2, nz, 2, nx, nyh), (*SEQ, *KV))
    placed = (P(KV, SEQ, None), P(KV, SEQ, None), P(KV, SEQ), P(), P())
    return jax.shard_map(
        functools.partial(body, sizes),
        mesh=torus,
        in_specs=placed,
        out_specs=(P(KV, SEQ), P(), P()),
        check_vma=False,
    )


def solution(mesh):
    return build(mesh, (mesh.shape["seq"] // 4, mesh.shape["kv"] // 2, 2))
```

time: 745 us -> 81.7 us (0.11)
  waiting for transfers between devices: 542 us -> 0 us
  Pallas kernels: 0 us -> 76.4 us
  matrix products: 74.3 us -> 0 us
  local copies, waits for them, and re-layouts: 42.7 us -> 4.36 us
  starting transfers between devices: 29.2 us -> 0 us
  other arithmetic: 26.4 us -> 0 us
  between operations: 13.9 us -> 0.65 us
    psum x1 -> x0, waiting for transfers between devices: 455 us -> none  [in_one(): so_far = lax.psum(jnp.concatenate([a.ravel() for a in arrays]), axis)]
    pallas_call x0 -> x1, Pallas kernels: none -> 76.4 us  [body(): pl.pallas_call(functools.partial(kernel, sizes), out_shape=(jax.ShapeDtyp...]
    dot_general x71 -> x0, matrix products: 74.3 us -> none  [the longest x64 70.5 us: score_tile(): lax.dot_general(row_block, key_block, (((1,), (1,)), ((), ())), preferred...]
    all_gather x2 -> x0, waiting for transfers between devices: 68.6 us -> none  [gather_in_order(): tiles = lax.all_gather(tiles, axes[k], axis=0, tiled=True)]
    all_to_all x2 -> x0, starting transfers between devices: 29 us -> none  [the longest x1 19.1 us: from_everyone(): return lax.all_to_all(copies, axis, split_axis=0, concat_axis=0, tiled=True)]
    dynamic_update_slice x64 -> x0, local copies, waits for them, and re-layouts: 26.3 us -> none  [absorb_one(): lax.dynamic_update_slice(rescaled, tile_mass, (jnp.int32(0), first_key //...]
    all_to_all x2 -> x0, waiting for transfers between devices: 19 us -> none  [the longest x1 13.9 us: sent_and_summed(): lax.all_to_all(tiles, axis, split_axis=0, concat_axis=0, tiled=True)]
    reduce_sum x69 -> x0, other arithmetic: 11.3 us -> none  [the longest x64 8.89 us: absorb_one(): tile_mass = jnp.sum(weights.reshape(row_count, local_blocks, BLOCK), axis=2)]
  transfers between devices with their start and end apart: 5 -> 0, of which waited for: 4 -> 0; matrix products, arithmetic and copies ran while one was open for 2% -> 0% of each run, Pallas kernels for 0% -> 0%
where the time goes in v1:
time: 81.7 us; the launch traced here: 81.4 us
  Pallas kernels  76.4 us (94%)
  local copies, waits for them, and re-layouts  4.36 us (5%)
    pallas_call x1, Pallas kernels, body(): pl.pallas_call(functools.partial(kernel, sizes), out_shape=(jax.ShapeDtyp...  76.4 us
    unnamed x5, local copies, waits for them, and re-layouts  4.36 us

profile of v1, /device:TPU:1, one launch (start us, length us, event | category | flops | bytes accessed | tf_op | source)
XLA Modules:
  0.0 81.4 jit_solution(7390812681637473988)
XLA Ops:
  0.6 76.4 %shard_map.76 = (f32[8,8]{1,0:T(8,128)}, f32[128,128]{1,0:T(8,128)}, f32[384,128]{1,0:T(8,128)}) custom-call(bf16[8,256,128]{2,1,0:T(8,128)(2,1)} %q_ref.1, bf16[1,256,128]{2,1,0:T(8,128)(2,1)} %k_ref.1, s32[8,8]{1,0:T(8,128)} %samples_ref.1, f32[128,128]{1,0:T(8,128)} %wq_ref.1, f32[384,128]{1,0:T(8,128)} %wk_ref.1), custom_call_target="tpu_custom_call" | custom-call | tf_op jit(solution)/shard_map/pallas_call | solution.py:411
  77.1 0.0 copy-start
  77.1 0.7 copy-done
  77.8 0.6 copy.11
  78.4 1.5 %copy.12 = f32[128,128]{1,0:T(8,128)} copy(f32[128,128]{1,0:T(8,128)} %get-tuple-element.7) | data formatting | bytes 131072
  79.8 1.6 %copy.13 = f32[384,128]{1,0:T(8,128)} copy(f32[384,128]{1,0:T(8,128)} %get-tuple-element.8) | data formatting | bytes 393216
Async XLA Ops:
  77.1 0.7 copy-start

commit v2 on v1

v2 whole, which is shorter than its diff:
```python
import functools
import math

import jax
import jax.numpy as jnp
from jax import lax
from jax.experimental import pallas as pl
from jax.experimental.pallas import tpu as pltpu
from jax.sharding import Mesh
from jax.sharding import PartitionSpec as P

BLOCK = 128
MESH = pl.DeviceIdType.MESH
LOW = -1e30
highest = lax.Precision.HIGHEST
NN = (((1,), (0,)), ((), ()))
NT = (((1,), (1,)), ((), ()))
TN = (((0,), (0,)), ((), ()))


def dot32(a, b, dims=NN):
    return lax.dot_general(a, b, dims, precision=highest, preferred_element_type=jnp.float32)


def partner(place, apart, size):
    if apart == 0:
        return place
    if size == 2:
        return 1 - place
    return (place + 1 - 2 * (place % 2), (place + 2) % 4, 3 - place)[apart - 1]


def kernel(
    sizes,
    q_hbm,
    k_hbm,
    samples_hbm,
    wq_hbm,
    wk_hbm,
    loss_ref,
    total_ref,
    q_ref,
    keys,
    samples_ref,
    wq_ref,
    wk_ref,
    pooled,
    queries,
    packed,
    returned,
    part,
    from_core,
    chip_sum,
    from_xy,
    xy_sum,
    from_z,
    z_sum,
    xy_all,
    load_sem,
    query_send,
    query_recv,
    pool_send,
    pool_recv,
    back_send,
    back_recv,
    slice_send,
    slice_recv,
    core_send,
    core_recv,
    sum_send,
    sum_recv,
    all_send,
    all_recv,
    z_send,
    z_recv,
):
    nz, nx, nyh = sizes
    ny = 2 * nyh
    direct = nz // 4
    z, yl, c = lax.axis_index("z"), lax.axis_index("yl"), lax.axis_index("c")
    x, yh = lax.axis_index("x"), lax.axis_index("yh")
    y = 2 * yh + yl
    started = []

    def send(src, dst, send_sem, recv_sem, target):
        copy = pltpu.make_async_remote_copy(
            src_ref=src,
            dst_ref=dst,
            send_sem=send_sem,
            recv_sem=recv_sem,
            device_id=target,
            device_id_type=MESH,
        )
        copy.start()
        started.append(copy)
        return copy

    def along_z(step):
        return {"z": (z + step + nz) % nz}

    def in_slice(i):
        return {"yl": partner(yl, i // 2, 2), "c": partner(c, i % 2, 2)}

    def along_xy(n):
        other = partner(y, n % ny, ny)
        return {"x": partner(x, n // ny, nx), "yh": other // 2, "yl": other % 2}

    hops = (0, 1, 2, 1)
    others_xy = sorted(range(1, nx * ny), key=lambda n: -hops[n // ny] - hops[n % ny])
    other_core = {"c": 1 - c}

    near = [along_z(sign * d) for d in range(direct, 0, -1) for sign in (1, -1)]
    near += [along_xy(n) for n in others_xy]
    near += [in_slice(3), other_core]
    barrier = pltpu.get_barrier_semaphore()
    for target in near:
        pl.semaphore_signal(barrier, inc=1, device_id=target, device_id_type=MESH)

    loads = [
        pltpu.make_async_copy(src, dst, load_sem.at[n])
        for n, (src, dst) in enumerate(
            (
                (samples_hbm, samples_ref),
                (q_hbm, q_ref),
                (k_hbm.at[0], keys.at[0]),
                (wq_hbm, wq_ref),
                (wk_hbm, wk_ref),
            )
        )
    ]
    for load in loads:
        load.start()

    loads[0].wait()
    shard = (yl * nz + z) * 2 + c
    local = (samples_ref[...] - shard * (2 * BLOCK)).astype(jnp.float32)
    spread = jnp.concatenate([jnp.broadcast_to(local[h : h + 1], (8, 8)) for h in range(8)], axis=0)
    lanes8 = lax.broadcasted_iota(jnp.int32, (64, 8), 1)
    rows8 = lax.broadcasted_iota(jnp.int32, (64, 8), 0) % 8
    column = jnp.sum(jnp.where(lanes8 == rows8, spread, 0.0), axis=1, keepdims=True)
    tokens = lax.broadcasted_iota(jnp.int32, (8, 2 * BLOCK), 1)
    query_rows, pooled_rows = [], []
    loads[1].wait()
    for h in range(8):
        place = column[8 * h : 8 * h + 8].astype(jnp.int32)
        chosen = jnp.where(tokens == place, 1.0, 0.0)
        block = jnp.where(tokens // BLOCK == place // BLOCK, 1.0, 0.0)
        both = lax.dot_general(
            jnp.concatenate([chosen, block], axis=0).astype(jnp.bfloat16),
            q_ref[h],
            NN,
            preferred_element_type=jnp.float32,
        )
        query_rows.append(both[:8])
        pooled_rows.append(both[8:] * (1.0 / BLOCK))
    queries[0] = jnp.concatenate(query_rows, axis=0).astype(jnp.bfloat16)

    loads[2].wait()
    own = keys[0].astype(jnp.float32)
    blocks = (own[:BLOCK], own[BLOCK:])
    pooled[0, 0] = jnp.concatenate(
        [jnp.max(b, axis=0, keepdims=True) for b in blocks]
        + [jnp.min(b, axis=0, keepdims=True) for b in blocks]
        + [jnp.sum(b, axis=0, keepdims=True) * (1.0 / BLOCK) for b in blocks]
        + [jnp.zeros((2, own.shape[1]), jnp.float32)],
        axis=0,
    )

    pl.semaphore_wait(barrier, len(near))

    arrivals = {}

    def pass_on(held, step):
        at = (held + step + nz) % nz
        target = along_z(step)
        arrivals["query", at] = send(
            queries.at[held], queries.at[at], query_send.at[at], query_recv.at[at], target
        )
        arrivals["pool", at] = send(
            pooled.at[0, held], pooled.at[0, at], pool_send.at[at], pool_recv.at[at], target
        )

    for d in range(direct, 0, -1):
        for sign in (1, -1):
            pass_on(0, sign * d)
    keys_here = [
        send(
            keys.at[0],
            keys.at[i],
            slice_send.at[0, i - 1],
            slice_recv.at[0, i - 1],
            in_slice(i),
        )
        for i in (2, 3, 1)
    ]
    pooled_rows = jnp.concatenate(pooled_rows + [jnp.zeros((64, BLOCK), jnp.float32)], axis=0)
    loads[3].wait()
    gate_rows = dot32(pooled_rows, wq_ref[...])
    lanes = lax.broadcasted_iota(jnp.int32, (1, 256), 1)
    eye = lax.broadcasted_iota(jnp.int32, (64, 256), 0) == lax.broadcasted_iota(
        jnp.int32, (64, 256), 1
    )
    places = jnp.sum(jnp.where(eye, column, 0.0), axis=0, keepdims=True).astype(jnp.int32)
    places = jnp.where(lanes < 64, places, 2 * BLOCK - 1)

    for sign, last in ((1, direct), (-1, direct - 1)):
        held = (sign * direct + nz) % nz
        arrivals["query", held].wait_recv()
        arrivals["pool", held].wait_recv()
        for step in range(last, 0, -1):
            pass_on(held, sign * step)
    waited = {0, direct, nz - direct}

    for copy in keys_here:
        copy.wait_recv()
    exponent = math.log2(math.e) / math.sqrt(BLOCK)
    first = lax.broadcasted_iota(jnp.int32, (8, BLOCK), 1) < 64
    returns = {}

    def score(slots):
        for at in slots:
            if at not in waited:
                arrivals["query", at].wait_recv()
        rows = queries[slots[0] : slots[0] + 4].reshape(256, BLOCK)
        tops, sums = [], []
        for i in range(4):
            scores = lax.dot_general(keys[i], rows, NT, preferred_element_type=jnp.float32)
            if i == 0 and slots[0] == 0:
                token = lax.broadcasted_iota(jnp.int32, scores.shape, 0)
                scores = jnp.where(token <= places, scores, LOW)
            for b in range(2):
                block_scores = scores[b * BLOCK : (b + 1) * BLOCK]
                highest_score = jnp.max(block_scores, axis=0, keepdims=True)
                weights = jnp.exp2((block_scores - highest_score) * exponent)
                tops.append(highest_score)
                sums.append(jnp.sum(weights, axis=0, keepdims=True))
        tops = jnp.concatenate(tops, axis=0)
        sums = jnp.concatenate(sums, axis=0)
        for pair in range(2):
            top = tops[:, pair * BLOCK : (pair + 1) * BLOCK]
            mass = sums[:, pair * BLOCK : (pair + 1) * BLOCK]
            at = slots[0] + 2 * pair
            packed[at] = jnp.where(first, top, pltpu.roll(mass, 64, 1))
            packed[at + 1] = jnp.where(first, pltpu.roll(top, 64, 1), mass)
        for at in slots:
            if at:
                back = nz - at
                returns[back] = send(
                    packed.at[at],
                    returned.at[back],
                    back_send.at[back],
                    back_recv.at[back],
                    along_z(-at),
                )

    groups = [tuple(range(4 * g, 4 * g + 4)) for g in range(nz // 4)]
    if nz == 16:
        groups = [groups[0], groups[3], groups[1], groups[2]]
    for group in groups:
        score(group)
    returned[0] = packed[0]

    for at in range(1, nz):
        if at not in waited:
            arrivals["pool", at].wait_recv()
    pooled_here = [
        send(
            pooled.at[0],
            pooled.at[i],
            slice_send.at[1, i - 1],
            slice_recv.at[1, i - 1],
            in_slice(i),
        )
        for i in (2, 3, 1)
    ]
    loads[4].wait()
    for copy in pooled_here:
        copy.wait_recv()

    nb = 8 * nz
    pooled_keys = jnp.concatenate(
        [
            jnp.concatenate([pooled[i, :, 2 * kind + b, :] for kind in range(3)], axis=1)
            for i in range(4)
            for b in range(2)
        ],
        axis=0,
    )
    gate_key = dot32(pooled_keys, wk_ref[...])
    gate_scale = 1.0 / math.sqrt(BLOCK)
    logits = dot32(gate_key, gate_rows, NT) * gate_scale
    order = lax.broadcasted_iota(jnp.int32, (nb, BLOCK), 0)
    lane = lax.broadcasted_iota(jnp.int32, (nb, BLOCK), 1)
    i_of = order // (2 * nz)
    b_of = order // nz % 2
    z_of = (z - order % nz + nz) % nz
    yl_of = (yl + i_of // 2) % 2
    c_of = (c + i_of % 2) % 2
    block_of = ((yl_of * nz + z_of) * 2 + c_of) * 2 + b_of
    own_block = 2 * shard + places[:, :BLOCK] // BLOCK
    allowed = block_of <= own_block
    logit_top = jnp.max(jnp.where(allowed, logits, LOW), axis=0, keepdims=True)
    gate_weights = jnp.where(allowed, jnp.exp(logits - logit_top), 0.0)
    gate_total = jnp.sum(gate_weights, axis=0, keepdims=True)
    log_total = logit_top + jnp.log(gate_total)
    gate = gate_weights / gate_total

    for back in sorted(returns):
        returns[back].wait_recv()
    pairs = jnp.concatenate([returned[:, r, :] for r in range(8)], axis=0)
    sums = pltpu.roll(pairs, 64, 1)
    row_top = jnp.max(jnp.where(allowed, pairs, LOW), axis=0, keepdims=True)
    masses = jnp.where(allowed, sums * jnp.exp2((pairs - row_top) * exponent), 0.0)
    teacher = masses / jnp.sum(masses, axis=0, keepdims=True)
    losses = log_total - jnp.sum(jnp.where(allowed, teacher * logits, 0.0), axis=0, keepdims=True)
    delta = jnp.where(allowed & (lane < 64), (gate - teacher) * gate_scale, 0.0)

    block_query = dot32(delta, pooled_rows)
    local_sum = dot32(block_query, pooled_keys, TN)
    part[0] = local_sum[:, :256]
    part[1, :, :BLOCK] = local_sum[:, 256:]
    part[1, :, BLOCK:] = jnp.zeros((BLOCK, BLOCK), jnp.float32)
    copy = send(part.at[1 - c], from_core, core_send.at[0], core_recv.at[0], other_core)
    head_of = lax.broadcasted_iota(jnp.int32, (8, BLOCK), 1) // 8
    head = lax.broadcasted_iota(jnp.int32, (8, BLOCK), 0)
    row_of = lax.broadcasted_iota(jnp.int32, (BLOCK, BLOCK), 0) % 8
    row = lax.broadcasted_iota(jnp.int32, (BLOCK, BLOCK), 1)
    by_head = jnp.where(head_of == head, jnp.broadcast_to(losses, (8, BLOCK)), 0.0)
    loss_ref[...] = dot32(by_head, jnp.where(row_of == row, 1.0, 0.0))[:, :8]
    copy.wait_recv()
    chip_sum[...] = part[c] + from_core[...]

    rows_xy = BLOCK // (nx * ny)

    def rows_of(n):
        at = partner(x, n // ny, nx) * ny + partner(y, n % ny, ny)
        return pl.ds(pl.multiple_of(at * rows_xy, rows_xy), rows_xy)

    copies = [
        send(chip_sum.at[rows_of(n)], from_xy.at[n], sum_send.at[n], sum_recv.at[n], along_xy(n))
        for n in others_xy
    ]
    total = chip_sum[rows_of(0)]
    for copy, n in reversed(list(zip(copies, others_xy))):
        copy.wait_recv()
        total = total + from_xy[n]
    xy_sum[...] = total

    far_first = sorted(range(1, nz), key=lambda d: -min(d, nz - d))
    copies = [
        send(xy_sum, from_z.at[z], z_send.at[d], z_recv.at[d], along_z(d)) for d in far_first
    ]
    from_z[z] = total
    for copy in copies:
        copy.wait_recv()
    total = from_z[0]
    for i in range(1, nz):
        total = total + from_z[i]

    z_sum[...] = total
    copies = [
        send(z_sum, xy_all.at[rows_of(0)], all_send.at[n], all_recv.at[n], along_xy(n))
        for n in others_xy
    ]
    xy_all[rows_of(0)] = total
    for copy in copies:
        copy.wait_recv()
    copy = send(xy_all, total_ref.at[c], core_send.at[1], core_recv.at[1], other_core)
    total_ref[c] = xy_all[...]
    copy.wait_recv()
    for copy in started:
        copy.wait_send()


def finish(loss_ref, total_ref, wq_ref, wk_ref, row_loss_ref, query_grad_ref, key_grad_ref):
    total = jnp.concatenate([total_ref[0], total_ref[1, :, :BLOCK]], axis=1)
    query_grad_ref[...] = dot32(total, wk_ref[...])
    key_grad_ref[...] = dot32(total, wq_ref[...], TN)
    row_loss_ref[...] = loss_ref[...]


def body(sizes, queries, key_states, samples, query_gate_weight, key_gate_weight):
    nz, nx, nyh = sizes
    nxy = 2 * nx * nyh
    rows_xy = BLOCK // nxy
    f32, bf16 = jnp.float32, jnp.bfloat16
    dma = pltpu.SemaphoreType.DMA
    vmem = pl.BlockSpec(memory_space=pltpu.VMEM)
    losses, total = pl.pallas_call(
        functools.partial(kernel, sizes),
        out_shape=(
            jax.ShapeDtypeStruct((8, 8), f32),
            jax.ShapeDtypeStruct((2, BLOCK, 256), f32),
        ),
        in_specs=[pl.BlockSpec(memory_space=pl.ANY)] * 5,
        out_specs=(vmem,) * 2,
        scratch_shapes=[
            pltpu.VMEM((8, 2 * BLOCK, BLOCK), bf16),
            pltpu.VMEM((4, 2 * BLOCK, BLOCK), bf16),
            pltpu.VMEM((8, 8), jnp.int32),
            pltpu.VMEM((BLOCK, BLOCK), f32),
            pltpu.VMEM((3 * BLOCK, BLOCK), f32),
            pltpu.VMEM((4, nz, 8, BLOCK), f32),
            pltpu.VMEM((nz, 64, BLOCK), bf16),
            pltpu.VMEM((nz, 8, BLOCK), f32),
            pltpu.VMEM((nz, 8, BLOCK), f32),
            pltpu.VMEM((2, BLOCK, 256), f32),
            pltpu.VMEM((BLOCK, 256), f32),
            pltpu.VMEM((BLOCK, 256), f32),
            pltpu.VMEM((nxy, rows_xy, 256), f32),
            pltpu.VMEM((rows_xy, 256), f32),
            pltpu.VMEM((nz, rows_xy, 256), f32),
            pltpu.VMEM((rows_xy, 256), f32),
            pltpu.VMEM((BLOCK, 256), f32),
            dma((5,)),
            dma((nz,)),
            dma((nz,)),
            dma((nz,)),
            dma((nz,)),
            dma((nz,)),
            dma((nz,)),
            dma((2, 3)),
            dma((2, 3)),
            dma((2,)),
            dma((2,)),
            dma((nxy,)),
            dma((nxy,)),
            dma((nxy,)),
            dma((nxy,)),
            dma((nz,)),
            dma((nz,)),
        ],
        compiler_params=pltpu.CompilerParams(collective_id=0, has_side_effects=True),
    )(queries, key_states, samples, query_gate_weight, key_gate_weight)
    return pl.pallas_call(
        finish,
        out_shape=(
            jax.ShapeDtypeStruct((8, 8), f32),
            jax.ShapeDtypeStruct((BLOCK, BLOCK), f32),
            jax.ShapeDtypeStruct((3 * BLOCK, BLOCK), f32),
        ),
        in_specs=[vmem] * 4,
        out_specs=(vmem,) * 3,
    )(losses, total, query_gate_weight, key_gate_weight)


SEQ = ("yl", "z", "c")
KV = ("x", "yh")


def build(mesh, sizes):
    nz, nx, nyh = sizes
    torus = Mesh(mesh.devices.reshape(2, nz, 2, nx, nyh), (*SEQ, *KV))
    placed = (P(KV, SEQ, None), P(KV, SEQ, None), P(KV, SEQ), P(), P())
    return jax.shard_map(
        functools.partial(body, sizes),
        mesh=torus,
        in_specs=placed,
        out_specs=(P(KV, SEQ), P(), P()),
        check_vma=False,
    )


def solution(mesh):
    return build(mesh, (mesh.shape["seq"] // 4, mesh.shape["kv"] // 2, 2))
```

time: 81.7 us -> 62.7 us (0.77)
  Pallas kernels: 76.4 us -> 61.9 us
  local copies, waits for them, and re-layouts: 4.36 us -> 0 us
    pallas_call x1, Pallas kernels: 76.4 us -> 59.7 us  [body(): pl.pallas_call(functools.partial(kernel, sizes), out_shape=(jax.ShapeDtyp...]
    unnamed x5 -> x0, local copies, waits for them, and re-layouts: 4.36 us -> none
    pallas_call x0 -> x1, Pallas kernels: none -> 2.2 us  [body(): pl.pallas_call(finish, out_shape=(jax.ShapeDtypeStruct((8, 8), f32), jax....]
where the time goes in v2:
time: 62.7 us; the launch traced here: 62.6 us
  Pallas kernels  61.9 us (99%)
  between operations  0.64 us (1%)
    pallas_call x1, Pallas kernels, body(): pl.pallas_call(functools.partial(kernel, sizes), out_shape=(jax.ShapeDtyp...  59.7 us
    pallas_call x1, Pallas kernels, body(): pl.pallas_call(finish, out_shape=(jax.ShapeDtypeStruct((8, 8), f32), jax....  2.2 us

profile of v2, /device:TPU:1, one launch (start us, length us, event | category | flops | bytes accessed | tf_op | source)
XLA Modules:
  0.0 62.6 jit_solution(11846740516773139918)
XLA Ops:
  0.6 59.7 %shard_map.76 = (f32[8,8]{1,0:T(8,128)}, f32[2,128,256]{2,1,0:T(8,128)}) custom-call(bf16[8,256,128]{2,1,0:T(8,128)(2,1)} %q_hbm.1, bf16[1,256,128]{2,1,0:T(8,128)(2,1)} %k_hbm.1, s32[8,8]{1,0:T(8,128)} %samples_hbm.1, f32[128,128]{1,0:T(8,128)} %wq_ref.1, f32[384,128]{1,0:T(8,128)} %wk_ref.1), custom_call_target="tpu_custom_call" | custom-call | tf_op jit(solution)/shard_map/pallas_call | solution.py:389
  60.4 2.2 %shard_map.77 = (f32[8,8]{1,0:T(8,128)}, f32[128,128]{1,0:T(8,128)}, f32[384,128]{1,0:T(8,128)}) custom-call(f32[8,8]{1,0:T(8,128)} %get-tuple-element.5.loss_ref, f32[2,128,256]{2,1,0:T(8,128)} %get-tuple-element.6.total_ref, f32[128,128]{1,0:T(8,128)} %wq_ref.1, f32[384,128]{1,0:T(8,128)} %wk_ref.1), custom_call_target="tpu_custom_call" | custom-call | tf_op jit(solution)/shard_map/pallas_call | solution.py:435

commit v3 on v2

v3 whole, which is shorter than its diff:
```python
import functools
import math

import jax
import jax.numpy as jnp
from jax import lax
from jax.experimental import pallas as pl
from jax.experimental.pallas import tpu as pltpu
from jax.sharding import Mesh
from jax.sharding import PartitionSpec as P

BLOCK = 128
MESH = pl.DeviceIdType.MESH
LOW = -1e30
highest = lax.Precision.HIGHEST
NN = (((1,), (0,)), ((), ()))
NT = (((1,), (1,)), ((), ()))
TN = (((0,), (0,)), ((), ()))
ROUTES = {
    4: ((1,), (1,), (), ((0, 1, 2, 3),)),
    8: ((1, 3), (1, -1), (1,), ((0, 1, 7, 3), (5, 4, 2, 6))),
    16: (
        (1, 2, 5),
        (3, 2, 1, -1, -2),
        (-2, -1, 1, 2),
        ((0, 1, 2, 15), (14, 5, 11, 4), (3, 12, 13, 6), (7, 8, 9, 10)),
    ),
}


def dot32(a, b, dims=NN):
    return lax.dot_general(a, b, dims, precision=highest, preferred_element_type=jnp.float32)


def partner(place, apart, size):
    if apart == 0:
        return place
    if size == 2:
        return 1 - place
    return (place + 1 - 2 * (place % 2), (place + 2) % 4, 3 - place)[apart - 1]


def kernel(
    sizes,
    q_hbm,
    k_hbm,
    samples_hbm,
    wq_hbm,
    wk_hbm,
    loss_ref,
    total_ref,
    wq_ref,
    wk_ref,
    q_ref,
    keys,
    samples_ref,
    pooled,
    queries,
    packed,
    returned,
    part,
    from_slice,
    slice_sum,
    from_z,
    z_sum,
    load_sem,
    query_send,
    query_recv,
    pool_send,
    pool_recv,
    keys_send,
    keys_recv,
    tile_send,
    tile_recv,
    back_send,
    back_recv,
    sum_send,
    sum_recv,
    z_send,
    z_recv,
    all_send,
    all_recv,
):
    nz, nx, nyh = sizes
    ny = 2 * nyh
    near_z, upper, lower, groups = ROUTES[nz]
    far = near_z[-1]
    z, yl, c = lax.axis_index("z"), lax.axis_index("yl"), lax.axis_index("c")
    x, yh = lax.axis_index("x"), lax.axis_index("yh")
    y = 2 * yh + yl
    def send(src, dst, send_sem, recv_sem, target):
        copy = pltpu.make_async_remote_copy(
            src_ref=src,
            dst_ref=dst,
            send_sem=send_sem,
            recv_sem=recv_sem,
            device_id=target,
            device_id_type=MESH,
        )
        copy.start()
        return copy

    def wait_for(ref, sem):
        pltpu.make_async_copy(ref, ref, sem).wait()

    def along_z(step):
        return {"z": (z + step + nz) % nz}

    def in_slice(i):
        return {"yl": partner(yl, i // 2, 2), "c": partner(c, i % 2, 2)}

    def along_xy(n):
        other = partner(y, n // 2 % ny, ny)
        return {
            "x": partner(x, n // (2 * ny), nx),
            "yh": other // 2,
            "yl": other % 2,
            "c": partner(c, n % 2, 2),
        }

    slice_size = 2 * nx * ny
    hops = (0, 1, 2, 1)
    others = sorted(
        range(1, slice_size), key=lambda n: -hops[n // (2 * ny)] - hops[n // 2 % ny]
    )
    touched = sorted({*near_z, *map(abs, upper), *map(abs, lower)}, reverse=True)
    near = [along_z(sign * d) for d in touched for sign in (1, -1)]
    near += [along_xy(n) for n in others]
    loads = [
        pltpu.make_async_copy(src, dst, load_sem.at[n])
        for n, (src, dst) in enumerate(
            (
                (samples_hbm, samples_ref),
                (q_hbm, q_ref),
                (k_hbm.at[0], keys.at[0]),
                (wq_hbm, wq_ref),
                (wk_hbm, wk_ref),
            )
        )
    ]
    for load in loads:
        load.start()

    barrier = pltpu.get_barrier_semaphore()
    for target in near:
        pl.semaphore_signal(barrier, inc=1, device_id=target, device_id_type=MESH)

    loads[2].wait()
    own = keys[0].astype(jnp.float32)
    blocks = (own[:BLOCK], own[BLOCK:])
    pooled[0, 0] = jnp.concatenate(
        [jnp.max(b, axis=0, keepdims=True) for b in blocks]
        + [jnp.min(b, axis=0, keepdims=True) for b in blocks]
        + [jnp.sum(b, axis=0, keepdims=True) * (1.0 / BLOCK) for b in blocks]
        + [jnp.zeros((2, own.shape[1]), jnp.float32)],
        axis=0,
    )

    loads[0].wait()
    shard = (yl * nz + z) * 2 + c
    local = (samples_ref[...] - shard * (2 * BLOCK)).astype(jnp.float32)
    spread = jnp.concatenate([jnp.broadcast_to(local[h : h + 1], (8, 8)) for h in range(8)], axis=0)
    lanes8 = lax.broadcasted_iota(jnp.int32, (64, 8), 1)
    rows8 = lax.broadcasted_iota(jnp.int32, (64, 8), 0) % 8
    column = jnp.sum(jnp.where(lanes8 == rows8, spread, 0.0), axis=1, keepdims=True)
    tokens = lax.broadcasted_iota(jnp.int32, (8, 2 * BLOCK), 1)
    query_rows, pooled_rows = [], []
    loads[1].wait()
    for h in range(8):
        place = column[8 * h : 8 * h + 8].astype(jnp.int32)
        chosen = jnp.where(tokens == place, 1.0, 0.0)
        block = jnp.where(tokens // BLOCK == place // BLOCK, 1.0, 0.0)
        both = lax.dot_general(
            jnp.concatenate([chosen, block], axis=0).astype(jnp.bfloat16),
            q_ref[h],
            NN,
            preferred_element_type=jnp.float32,
        )
        query_rows.append(both[:8])
        pooled_rows.append(both[8:] * (1.0 / BLOCK))
    queries[0] = jnp.concatenate(query_rows, axis=0).astype(jnp.bfloat16)

    pl.semaphore_wait(barrier, len(near))

    far_places = (far, nz - far)
    group_of = {at: g for g, group in enumerate(groups) for at in group}
    group_of.update({at: len(groups) + n for n, at in enumerate(far_places)})
    waits = [[at for at in group if at not in (0, *far_places)] for group in groups]

    def pass_pool(held, step):
        at = (held + step + nz) % nz
        send(
            pooled.at[0, held],
            pooled.at[0, at],
            pool_send,
            pool_recv.at[group_of[at]],
            along_z(step),
        )

    def pass_query(held, step):
        at = (held + step + nz) % nz
        send(
            queries.at[held],
            queries.at[at],
            query_send,
            query_recv.at[group_of[at]],
            along_z(step),
        )

    for d in reversed(near_z):
        for sign in (1, -1):
            pass_query(0, sign * d)
    for d in reversed(near_z):
        for sign in (1, -1):
            pass_pool(0, sign * d)
    for i in (2, 3, 1):
        send(keys.at[0], keys.at[i], keys_send, keys_recv, in_slice(i))
    pooled_rows = jnp.concatenate(pooled_rows + [jnp.zeros((64, BLOCK), jnp.float32)], axis=0)
    loads[3].wait()
    gate_rows = dot32(pooled_rows, wq_ref[...])
    lanes = lax.broadcasted_iota(jnp.int32, (1, 256), 1)
    eye = lax.broadcasted_iota(jnp.int32, (64, 256), 0) == lax.broadcasted_iota(
        jnp.int32, (64, 256), 1
    )
    places = jnp.sum(jnp.where(eye, column, 0.0), axis=0, keepdims=True).astype(jnp.int32)
    places = jnp.where(lanes < 64, places, 2 * BLOCK - 1)

    for pass_on, kept, recv in (
        (pass_query, queries, query_recv),
        (pass_pool, pooled.at[0], pool_recv),
    ):
        for held, steps in zip(far_places, (upper, lower)):
            wait_for(kept.at[held], recv.at[group_of[held]])
            for step in steps:
                pass_on(held, step)

    wait_for(keys.at[1:4], keys_recv)
    exponent = math.log2(math.e) / math.sqrt(BLOCK)
    first = lax.broadcasted_iota(jnp.int32, (8, BLOCK), 1) < 64

    def score(slots, waited):
        wait_for(queries.at[: len(waited)], query_recv.at[group_of[waited[0]]])
        rows = jnp.concatenate([queries[at] for at in slots], axis=0)
        tops, sums = [], []
        for i in range(4):
            scores = lax.dot_general(keys[i], rows, NT, preferred_element_type=jnp.float32)
            if i == 0 and slots[0] == 0:
                token = lax.broadcasted_iota(jnp.int32, scores.shape, 0)
                scores = jnp.where(token <= places, scores, LOW)
            for b in range(2):
                block_scores = scores[b * BLOCK : (b + 1) * BLOCK]
                highest_score = jnp.max(block_scores, axis=0, keepdims=True)
                weights = jnp.exp2((block_scores - highest_score) * exponent)
                tops.append(highest_score)
                sums.append(jnp.sum(weights, axis=0, keepdims=True))
        tops = jnp.concatenate(tops, axis=0)
        sums = jnp.concatenate(sums, axis=0)
        for pair in range(2):
            top = tops[:, pair * BLOCK : (pair + 1) * BLOCK]
            mass = sums[:, pair * BLOCK : (pair + 1) * BLOCK]
            packed[slots[2 * pair]] = jnp.where(first, top, pltpu.roll(mass, 64, 1))
            packed[slots[2 * pair + 1]] = jnp.where(first, pltpu.roll(top, 64, 1), mass)
        for at in slots:
            if at:
                back = nz - at
                send(packed.at[at], returned.at[back], back_send, back_recv, along_z(-at))

    for group, waited in zip(groups, waits):
        score(group, waited)
        wait_for(pooled.at[0, : len(waited)], pool_recv.at[group_of[waited[0]]])
        for at in group:
            for i in (2, 3, 1):
                send(pooled.at[0, at], pooled.at[i, at], tile_send, tile_recv, in_slice(i))
    returned[0] = packed[0]
    loads[4].wait()
    wait_for(pooled.at[1:4], tile_recv)

    nb = 8 * nz
    pooled_keys = jnp.concatenate(
        [
            jnp.concatenate([pooled[i, :, 2 * kind + b, :] for kind in range(3)], axis=1)
            for i in range(4)
            for b in range(2)
        ],
        axis=0,
    )
    gate_key = dot32(pooled_keys, wk_ref[...])
    gate_scale = 1.0 / math.sqrt(BLOCK)
    logits = dot32(gate_key, gate_rows, NT) * gate_scale
    order = lax.broadcasted_iota(jnp.int32, (nb, BLOCK), 0)
    lane = lax.broadcasted_iota(jnp.int32, (nb, BLOCK), 1)
    i_of = order // (2 * nz)
    b_of = order // nz % 2
    z_of = (z - order % nz + nz) % nz
    yl_of = (yl + i_of // 2) % 2
    c_of = (c + i_of % 2) % 2
    block_of = ((yl_of * nz + z_of) * 2 + c_of) * 2 + b_of
    own_block = 2 * shard + places[:, :BLOCK] // BLOCK
    allowed = block_of <= own_block
    logit_top = jnp.max(jnp.where(allowed, logits, LOW), axis=0, keepdims=True)
    gate_weights = jnp.where(allowed, jnp.exp(logits - logit_top), 0.0)
    gate_total = jnp.sum(gate_weights, axis=0, keepdims=True)
    log_total = logit_top + jnp.log(gate_total)
    gate = gate_weights / gate_total

    wait_for(returned.at[1:], back_recv)
    pairs = jnp.concatenate([returned[:, r, :] for r in range(8)], axis=0)
    sums = pltpu.roll(pairs, 64, 1)
    row_top = jnp.max(jnp.where(allowed, pairs, LOW), axis=0, keepdims=True)
    masses = jnp.where(allowed, sums * jnp.exp2((pairs - row_top) * exponent), 0.0)
    teacher = masses / jnp.sum(masses, axis=0, keepdims=True)
    losses = log_total - jnp.sum(jnp.where(allowed, teacher * logits, 0.0), axis=0, keepdims=True)
    delta = jnp.where(allowed & (lane < 64), (gate - teacher) * gate_scale, 0.0)

    block_query = dot32(delta, pooled_rows)
    local_sum = dot32(block_query, pooled_keys, TN)
    rows = BLOCK // slice_size
    for n in range(slice_size):
        for kind in range(3):
            part[n, kind] = local_sum[rows * n : rows * (n + 1), BLOCK * kind : BLOCK * (kind + 1)]

    def place_of(n):
        at = partner(x, n // (2 * ny), nx) * ny + partner(y, n // 2 % ny, ny)
        return 2 * at + partner(c, n % 2, 2)

    for n in others:
        send(part.at[place_of(n)], from_slice.at[n], sum_send, sum_recv, along_xy(n))
    head_of = lax.broadcasted_iota(jnp.int32, (8, BLOCK), 1) // 8
    head = lax.broadcasted_iota(jnp.int32, (8, BLOCK), 0)
    row_of = lax.broadcasted_iota(jnp.int32, (BLOCK, BLOCK), 0) % 8
    row = lax.broadcasted_iota(jnp.int32, (BLOCK, BLOCK), 1)
    by_head = jnp.where(head_of == head, jnp.broadcast_to(losses, (8, BLOCK)), 0.0)
    loss_ref[...] = dot32(by_head, jnp.where(row_of == row, 1.0, 0.0))[:, :8]
    total = part[place_of(0)]
    wait_for(from_slice.at[1:], sum_recv)
    for n in range(1, slice_size):
        total = total + from_slice[n]
    slice_sum[...] = total

    far_first = sorted(range(1, nz), key=lambda d: -min(d, nz - d))
    for d in far_first:
        send(slice_sum, from_z.at[z], z_send, z_recv, along_z(d))
    from_z[z] = total
    wait_for(from_z.at[1:], z_recv)
    total = from_z[0]
    for i in range(1, nz):
        total = total + from_z[i]

    z_sum[...] = total
    for n in others:
        send(z_sum, total_ref.at[place_of(0)], all_send, all_recv, along_xy(n))
    total_ref[place_of(0)] = total
    wait_for(queries.at[1:], query_send)
    wait_for(pooled.at[0, 1:], pool_send)
    wait_for(keys.at[1:], keys_send)
    wait_for(packed.at[1:], back_send)
    wait_for(pooled.at[1:], tile_send)
    wait_for(part.at[1:], sum_send)
    wait_for(from_z.at[1:], z_send)
    wait_for(from_slice.at[1:], all_send)
    wait_for(from_slice.at[1:], all_recv)


def finish(loss_ref, total_ref, wq_ref, wk_ref, row_loss_ref, query_grad_ref, key_grad_ref):
    total = jnp.concatenate(
        [
            jnp.concatenate([total_ref[n, kind] for n in range(total_ref.shape[0])], axis=0)
            for kind in range(3)
        ],
        axis=1,
    )
    query_grad_ref[...] = dot32(total, wk_ref[...])
    key_grad_ref[...] = dot32(total, wq_ref[...], TN)
    row_loss_ref[...] = loss_ref[...]


def body(sizes, queries, key_states, samples, query_gate_weight, key_gate_weight):
    nz, nx, nyh = sizes
    slice_size = 4 * nx * nyh
    tile = (3, BLOCK // slice_size, BLOCK)
    f32, bf16 = jnp.float32, jnp.bfloat16
    dma = pltpu.SemaphoreType.DMA
    vmem = pl.BlockSpec(memory_space=pltpu.VMEM)
    handed = pl.pallas_call(
        functools.partial(kernel, sizes),
        out_shape=(
            pltpu.VMEM((8, 8), f32),
            pltpu.VMEM((slice_size, *tile), f32),
            pltpu.VMEM((BLOCK, BLOCK), f32),
            pltpu.VMEM((3 * BLOCK, BLOCK), f32),
        ),
        in_specs=[pl.BlockSpec(memory_space=pl.ANY)] * 5,
        out_specs=(vmem,) * 4,
        scratch_shapes=[
            pltpu.VMEM((8, 2 * BLOCK, BLOCK), bf16),
            pltpu.VMEM((4, 2 * BLOCK, BLOCK), bf16),
            pltpu.VMEM((8, 8), jnp.int32),
            pltpu.VMEM((4, nz, 8, BLOCK), f32),
            pltpu.VMEM((nz, 64, BLOCK), bf16),
            pltpu.VMEM((nz, 8, BLOCK), f32),
            pltpu.VMEM((nz, 8, BLOCK), f32),
            pltpu.VMEM((slice_size, *tile), f32),
            pltpu.VMEM((slice_size, *tile), f32),
            pltpu.VMEM(tile, f32),
            pltpu.VMEM((nz, *tile), f32),
            pltpu.VMEM(tile, f32),
            dma((5,)),
            dma,
            dma((len(ROUTES[nz][3]) + 2,)),
            dma,
            dma((len(ROUTES[nz][3]) + 2,)),
        ]
        + [dma] * 12,
        compiler_params=pltpu.CompilerParams(collective_id=0, has_side_effects=True),
    )(queries, key_states, samples, query_gate_weight, key_gate_weight)
    return pl.pallas_call(
        finish,
        out_shape=(
            jax.ShapeDtypeStruct((8, 8), f32),
            jax.ShapeDtypeStruct((BLOCK, BLOCK), f32),
            jax.ShapeDtypeStruct((3 * BLOCK, BLOCK), f32),
        ),
        in_specs=[vmem] * 4,
        out_specs=(vmem,) * 3,
    )(*[pltpu.with_memory_space_constraint(a, pltpu.VMEM) for a in handed])


SEQ = ("yl", "z", "c")
KV = ("x", "yh")


def build(mesh, sizes):
    nz, nx, nyh = sizes
    torus = Mesh(mesh.devices.reshape(2, nz, 2, nx, nyh), (*SEQ, *KV))
    placed = (P(KV, SEQ, None), P(KV, SEQ, None), P(KV, SEQ), P(), P())
    return jax.shard_map(
        functools.partial(body, sizes),
        mesh=torus,
        in_specs=placed,
        out_specs=(P(KV, SEQ), P(), P()),
        check_vma=False,
    )


def solution(mesh):
    return build(mesh, (mesh.shape["seq"] // 4, mesh.shape["kv"] // 2, 2))
```

time: 62.7 us -> 57 us (0.909)
  Pallas kernels: 61.9 us -> 56.2 us
    pallas_call x1, Pallas kernels: 59.7 us -> 55 us  [body(): pl.pallas_call(functools.partial(kernel, sizes), out_shape=(pltpu.VMEM((8...]
    pallas_call x1, Pallas kernels: 2.2 us -> 1.16 us  [body(): pl.pallas_call(finish, out_shape=(jax.ShapeDtypeStruct((8, 8), f32), jax....]
where the time goes in v3:
time: 57 us; the launch traced here: 56.8 us
  Pallas kernels  56.2 us (99%)
  between operations  0.64 us (1%)
    pallas_call x1, Pallas kernels, body(): pl.pallas_call(functools.partial(kernel, sizes), out_shape=(pltpu.VMEM((8...  55 us
    pallas_call x1, Pallas kernels, body(): pl.pallas_call(finish, out_shape=(jax.ShapeDtypeStruct((8, 8), f32), jax....  1.16 us

profile of v3, /device:TPU:1, one launch (start us, length us, event | category | flops | bytes accessed | tf_op | source)
XLA Modules:
  0.0 56.8 jit_solution(4611512546442019915)
XLA Ops:
  0.6 55.0 %shard_map.76 = (f32[8,8]{1,0:T(8,128)S(1)}, f32[32,3,4,128]{3,2,1,0:T(4,128)S(1)}, f32[128,128]{1,0:T(8,128)S(1)}, f32[384,128]{1,0:T(8,128)S(1)}) custom-call(bf16[8,256,128]{2,1,0:T(8,128)(2,1)} %q_hbm.1, bf16[1,256,128]{2,1,0:T(8,128)(2,1)} %k_hbm.1, s32[8,8]{1,0:T(8,128)} %samples_hbm.1, f32[128,128]{1,0:T(8,128)} %wq_hbm.1, f32[384,128]{1,0:T(8,128)} %wk_hbm.1), custom_call_target="tpu_custom_call" | custom-call | tf_op jit(solution)/shard_map/pallas_call | solution.py:384
  55.7 1.2 %shard_map.77 = (f32[8,8]{1,0:T(8,128)}, f32[128,128]{1,0:T(8,128)}, f32[384,128]{1,0:T(8,128)}) custom-call(f32[8,8]{1,0:T(8,128)S(1)} %get-tuple-element.7.loss_ref, f32[32,3,4,128]{3,2,1,0:T(4,128)S(1)} %get-tuple-element.8.total_ref, f32[128,128]{1,0:T(8,128)S(1)} %get-tuple-element.9.wq_ref, f32[384,128]{1,0:T(8,128)S(1)} %get-tuple-element.10.wk_ref), custom_call_target="tpu_custom_call" | custom-call | tf_op jit(solution)/shard_map/pallas_call | solution.py:416

commit v4 on v3

--- a/solution.py
+++ b/solution.py
@@ -23,7 +23,7 @@
         (1, 2, 5),
         (3, 2, 1, -1, -2),
         (-2, -1, 1, 2),
-        ((0, 1, 2, 15), (14, 5, 11, 4), (3, 12, 13, 6), (7, 8, 9, 10)),
+        ((0, 1, 2, 15), (14, 5, 11, 6), (7, 8, 9, 10), (4, 3, 12, 13)),
     ),
 }
 
@@ -190,8 +190,8 @@
     def pass_pool(held, step):
         at = (held + step + nz) % nz
         send(
-            pooled.at[0, held],
-            pooled.at[0, at],
+            pooled.at[0, held, :6],
+            pooled.at[0, at, :6],
             pool_send,
             pool_recv.at[group_of[at]],
             along_z(step),
@@ -218,6 +218,7 @@
     pooled_rows = jnp.concatenate(pooled_rows + [jnp.zeros((64, BLOCK), jnp.float32)], axis=0)
     loads[3].wait()
     gate_rows = dot32(pooled_rows, wq_ref[...])
+    pooled_columns = pooled_rows.T
     lanes = lax.broadcasted_iota(jnp.int32, (1, 256), 1)
     eye = lax.broadcasted_iota(jnp.int32, (64, 256), 0) == lax.broadcasted_iota(
         jnp.int32, (64, 256), 1
@@ -230,7 +231,7 @@
         (pass_pool, pooled.at[0], pool_recv),
     ):
         for held, steps in zip(far_places, (upper, lower)):
-            wait_for(kept.at[held], recv.at[group_of[held]])
+            wait_for(kept.at[held] if kept is queries else kept.at[held, :6], recv.at[group_of[held]])
             for step in steps:
                 pass_on(held, step)
 
@@ -265,15 +266,23 @@
                 back = nz - at
                 send(packed.at[at], returned.at[back], back_send, back_recv, along_z(-at))
 
-    for group, waited in zip(groups, waits):
-        score(group, waited)
-        wait_for(pooled.at[0, : len(waited)], pool_recv.at[group_of[waited[0]]])
+    def share_tiles(group, waited):
+        wait_for(pooled.at[0, : len(waited), :6], pool_recv.at[group_of[waited[0]]])
         for at in group:
             for i in (2, 3, 1):
-                send(pooled.at[0, at], pooled.at[i, at], tile_send, tile_recv, in_slice(i))
+                send(
+                    pooled.at[0, at, :6], pooled.at[i, at, :6], tile_send, tile_recv, in_slice(i)
+                )
+
+    for n, (group, waited) in enumerate(zip(groups, waits)):
+        score(group, waited)
+        if n < len(groups) - 2:
+            share_tiles(group, waited)
+    for group, waited in list(zip(groups, waits))[-2:]:
+        share_tiles(group, waited)
     returned[0] = packed[0]
     loads[4].wait()
-    wait_for(pooled.at[1:4], tile_recv)
+    wait_for(pooled.at[1:4, :, :6], tile_recv)
 
     nb = 8 * nz
     pooled_keys = jnp.concatenate(
@@ -312,8 +321,8 @@
     losses = log_total - jnp.sum(jnp.where(allowed, teacher * logits, 0.0), axis=0, keepdims=True)
     delta = jnp.where(allowed & (lane < 64), (gate - teacher) * gate_scale, 0.0)
 
-    block_query = dot32(delta, pooled_rows)
-    local_sum = dot32(block_query, pooled_keys, TN)
+    block_query = dot32(pooled_columns, delta, NT)
+    local_sum = dot32(block_query, pooled_keys)
     rows = BLOCK // slice_size
     for n in range(slice_size):
         for kind in range(3):
@@ -351,10 +360,10 @@
         send(z_sum, total_ref.at[place_of(0)], all_send, all_recv, along_xy(n))
     total_ref[place_of(0)] = total
     wait_for(queries.at[1:], query_send)
-    wait_for(pooled.at[0, 1:], pool_send)
+    wait_for(pooled.at[0, 1:, :6], pool_send)
     wait_for(keys.at[1:], keys_send)
     wait_for(packed.at[1:], back_send)
-    wait_for(pooled.at[1:], tile_send)
+    wait_for(pooled.at[1:, :, :6], tile_send)
     wait_for(part.at[1:], sum_send)
     wait_for(from_z.at[1:], z_send)
     wait_for(from_slice.at[1:], all_send)

time: 57 us -> 56.3 us (0.988)
  Pallas kernels: 56.2 us -> 55.5 us
    pallas_call x1, Pallas kernels: 55 us -> 54.4 us  [body(): pl.pallas_call(functools.partial(kernel, sizes), out_shape=(pltpu.VMEM((8...]
where the time goes in v4:
time: 56.3 us; the launch traced here: 56.2 us
  Pallas kernels  55.5 us (99%)
  between operations  0.64 us (1%)
    pallas_call x1, Pallas kernels, body(): pl.pallas_call(functools.partial(kernel, sizes), out_shape=(pltpu.VMEM((8...  54.4 us
    pallas_call x1, Pallas kernels, body(): pl.pallas_call(finish, out_shape=(jax.ShapeDtypeStruct((8, 8), f32), jax....  1.16 us

profile of v4, /device:TPU:1, one launch (start us, length us, event | category | flops | bytes accessed | tf_op | source)
XLA Modules:
  0.0 56.2 jit_solution(7941949795797205951)
XLA Ops:
  0.6 54.4 %shard_map.76 = (f32[8,8]{1,0:T(8,128)S(1)}, f32[32,3,4,128]{3,2,1,0:T(4,128)S(1)}, f32[128,128]{1,0:T(8,128)S(1)}, f32[384,128]{1,0:T(8,128)S(1)}) custom-call(bf16[8,256,128]{2,1,0:T(8,128)(2,1)} %q_hbm.1, bf16[1,256,128]{2,1,0:T(8,128)(2,1)} %k_hbm.1, s32[8,8]{1,0:T(8,128)} %samples_hbm.1, f32[128,128]{1,0:T(8,128)} %wq_hbm.1, f32[384,128]{1,0:T(8,128)} %wk_hbm.1), custom_call_target="tpu_custom_call" | custom-call | tf_op jit(solution)/shard_map/pallas_call | solution.py:393
  55.0 1.2 %shard_map.77 = (f32[8,8]{1,0:T(8,128)}, f32[128,128]{1,0:T(8,128)}, f32[384,128]{1,0:T(8,128)}) custom-call(f32[8,8]{1,0:T(8,128)S(1)} %get-tuple-element.7.loss_ref, f32[32,3,4,128]{3,2,1,0:T(4,128)S(1)} %get-tuple-element.8.total_ref, f32[128,128]{1,0:T(8,128)S(1)} %get-tuple-element.9.wq_ref, f32[384,128]{1,0:T(8,128)S(1)} %get-tuple-element.10.wk_ref), custom_call_target="tpu_custom_call" | custom-call | tf_op jit(solution)/shard_map/pallas_call | solution.py:425

commit v5 on v4

--- a/solution.py
+++ b/solution.py
@@ -20,10 +20,10 @@
     4: ((1,), (1,), (), ((0, 1, 2, 3),)),
     8: ((1, 3), (1, -1), (1,), ((0, 1, 7, 3), (5, 4, 2, 6))),
     16: (
-        (1, 2, 5),
-        (3, 2, 1, -1, -2),
-        (-2, -1, 1, 2),
-        ((0, 1, 2, 15), (14, 5, 11, 6), (7, 8, 9, 10), (4, 3, 12, 13)),
+        (1, 2, 4),
+        (4, 3, 2, 1, -1),
+        (-3, -2, -1, 1),
+        ((0, 1, 2, 15), (14, 4, 12, 5), (6, 7, 8, 9), (10, 11, 3, 13)),
     ),
 }
 

time: 56.3 us -> 54.7 us (0.972)
  Pallas kernels: 55.5 us -> 53.9 us
    pallas_call x1, Pallas kernels: 54.4 us -> 52.7 us  [body(): pl.pallas_call(functools.partial(kernel, sizes), out_shape=(pltpu.VMEM((8...]
where the time goes in v5:
time: 54.7 us; the launch traced here: 54.5 us
  Pallas kernels  53.9 us (99%)
  between operations  0.64 us (1%)
    pallas_call x1, Pallas kernels, body(): pl.pallas_call(functools.partial(kernel, sizes), out_shape=(pltpu.VMEM((8...  52.7 us
    pallas_call x1, Pallas kernels, body(): pl.pallas_call(finish, out_shape=(jax.ShapeDtypeStruct((8, 8), f32), jax....  1.16 us

profile of v5, /device:TPU:1, one launch (start us, length us, event | category | flops | bytes accessed | tf_op | source)
XLA Modules:
  0.0 54.5 jit_solution(1637559705393390012)
XLA Ops:
  0.6 52.7 %shard_map.76 = (f32[8,8]{1,0:T(8,128)S(1)}, f32[32,3,4,128]{3,2,1,0:T(4,128)S(1)}, f32[128,128]{1,0:T(8,128)S(1)}, f32[384,128]{1,0:T(8,128)S(1)}) custom-call(bf16[8,256,128]{2,1,0:T(8,128)(2,1)} %q_hbm.1, bf16[1,256,128]{2,1,0:T(8,128)(2,1)} %k_hbm.1, s32[8,8]{1,0:T(8,128)} %samples_hbm.1, f32[128,128]{1,0:T(8,128)} %wq_hbm.1, f32[384,128]{1,0:T(8,128)} %wk_hbm.1), custom_call_target="tpu_custom_call" | custom-call | tf_op jit(solution)/shard_map/pallas_call | solution.py:393
  53.4 1.2 %shard_map.77 = (f32[8,8]{1,0:T(8,128)}, f32[128,128]{1,0:T(8,128)}, f32[384,128]{1,0:T(8,128)}) custom-call(f32[8,8]{1,0:T(8,128)S(1)} %get-tuple-element.7.loss_ref, f32[32,3,4,128]{3,2,1,0:T(4,128)S(1)} %get-tuple-element.8.total_ref, f32[128,128]{1,0:T(8,128)S(1)} %get-tuple-element.9.wq_ref, f32[384,128]{1,0:T(8,128)S(1)} %get-tuple-element.10.wk_ref), custom_call_target="tpu_custom_call" | custom-call | tf_op jit(solution)/shard_map/pallas_call | solution.py:425

commit v6 on v5

--- a/solution.py
+++ b/solution.py
@@ -323,51 +323,67 @@
 
     block_query = dot32(pooled_columns, delta, NT)
     local_sum = dot32(block_query, pooled_keys)
-    rows = BLOCK // slice_size
-    for n in range(slice_size):
+    chunks = nx * ny
+    rows = BLOCK // chunks
+    for n in range(chunks):
         for kind in range(3):
             part[n, kind] = local_sum[rows * n : rows * (n + 1), BLOCK * kind : BLOCK * (kind + 1)]
 
     def place_of(n):
-        at = partner(x, n // (2 * ny), nx) * ny + partner(y, n // 2 % ny, ny)
-        return 2 * at + partner(c, n % 2, 2)
-
-    for n in others:
-        send(part.at[place_of(n)], from_slice.at[n], sum_send, sum_recv, along_xy(n))
+        return partner(x, n // (2 * ny), nx) * ny + partner(y, n // 2 % ny, ny)
+
+    for core in (0, 1):
+
+        @pl.when(c == core)
+        def share():
+            for n in others:
+                if n % 2 != core:
+                    send(part.at[place_of(n)], from_slice.at[n], sum_send, sum_recv, along_xy(n))
+
     head_of = lax.broadcasted_iota(jnp.int32, (8, BLOCK), 1) // 8
     head = lax.broadcasted_iota(jnp.int32, (8, BLOCK), 0)
     row_of = lax.broadcasted_iota(jnp.int32, (BLOCK, BLOCK), 0) % 8
     row = lax.broadcasted_iota(jnp.int32, (BLOCK, BLOCK), 1)
     by_head = jnp.where(head_of == head, jnp.broadcast_to(losses, (8, BLOCK)), 0.0)
     loss_ref[...] = dot32(by_head, jnp.where(row_of == row, 1.0, 0.0))[:, :8]
-    total = part[place_of(0)]
-    wait_for(from_slice.at[1:], sum_recv)
-    for n in range(1, slice_size):
-        total = total + from_slice[n]
-    slice_sum[...] = total
-
     far_first = sorted(range(1, nz), key=lambda d: -min(d, nz - d))
-    for d in far_first:
-        send(slice_sum, from_z.at[z], z_send, z_recv, along_z(d))
-    from_z[z] = total
-    wait_for(from_z.at[1:], z_recv)
-    total = from_z[0]
-    for i in range(1, nz):
-        total = total + from_z[i]
-
-    z_sum[...] = total
-    for n in others:
-        send(z_sum, total_ref.at[place_of(0)], all_send, all_recv, along_xy(n))
-    total_ref[place_of(0)] = total
+
+    @pl.when(c == 1)
+    def own():
+        wait_for(from_slice.at[1:], sum_recv)
+        total = part[place_of(0)]
+        for n in range(1, slice_size):
+            total = total + from_slice[n]
+        slice_sum[...] = total
+        for d in far_first:
+            send(slice_sum, from_z.at[z], z_send, z_recv, along_z(d))
+        from_z[z] = total
+        wait_for(from_z.at[1:], z_recv)
+        total = from_z[0]
+        for i in range(1, nz):
+            total = total + from_z[i]
+        z_sum[...] = total
+        for n in others:
+            send(z_sum, total_ref.at[place_of(0)], all_send, all_recv, along_xy(n))
+        total_ref[place_of(0)] = total
+
     wait_for(queries.at[1:], query_send)
     wait_for(pooled.at[0, 1:, :6], pool_send)
     wait_for(keys.at[1:], keys_send)
     wait_for(packed.at[1:], back_send)
     wait_for(pooled.at[1:, :, :6], tile_send)
-    wait_for(part.at[1:], sum_send)
-    wait_for(from_z.at[1:], z_send)
-    wait_for(from_slice.at[1:], all_send)
-    wait_for(from_slice.at[1:], all_recv)
+
+    @pl.when(c == 0)
+    def end_core_0():
+        wait_for(part, sum_send)
+        wait_for(part, all_recv)
+
+    @pl.when(c == 1)
+    def end_core_1():
+        wait_for(part.at[1:], sum_send)
+        wait_for(from_z.at[1:], z_send)
+        wait_for(from_slice.at[1:], all_send)
+        wait_for(part.at[1:], all_recv)
 
 
 def finish(loss_ref, total_ref, wq_ref, wk_ref, row_loss_ref, query_grad_ref, key_grad_ref):
@@ -386,7 +402,8 @@
 def body(sizes, queries, key_states, samples, query_gate_weight, key_gate_weight):
     nz, nx, nyh = sizes
     slice_size = 4 * nx * nyh
-    tile = (3, BLOCK // slice_size, BLOCK)
+    chunks = slice_size // 2
+    tile = (3, BLOCK // chunks, BLOCK)
     f32, bf16 = jnp.float32, jnp.bfloat16
     dma = pltpu.SemaphoreType.DMA
     vmem = pl.BlockSpec(memory_space=pltpu.VMEM)
@@ -394,7 +411,7 @@
         functools.partial(kernel, sizes),
         out_shape=(
             pltpu.VMEM((8, 8), f32),
-            pltpu.VMEM((slice_size, *tile), f32),
+            pltpu.VMEM((chunks, *tile), f32),
             pltpu.VMEM((BLOCK, BLOCK), f32),
             pltpu.VMEM((3 * BLOCK, BLOCK), f32),
         ),
@@ -408,7 +425,7 @@
             pltpu.VMEM((nz, 64, BLOCK), bf16),
             pltpu.VMEM((nz, 8, BLOCK), f32),
             pltpu.VMEM((nz, 8, BLOCK), f32),
-            pltpu.VMEM((slice_size, *tile), f32),
+            pltpu.VMEM((chunks, *tile), f32),
             pltpu.VMEM((slice_size, *tile), f32),
             pltpu.VMEM(tile, f32),
             pltpu.VMEM((nz, *tile), f32),

time: 54.7 us -> 53.8 us (0.984)
  Pallas kernels: 53.9 us -> 53 us
    pallas_call x1, Pallas kernels: 52.7 us -> 51.8 us  [body(): pl.pallas_call(functools.partial(kernel, sizes), out_shape=(pltpu.VMEM((8...]
where the time goes in v6:
time: 53.8 us; the launch traced here: 53.6 us
  Pallas kernels  53 us (99%)
  between operations  0.64 us (1%)
    pallas_call x1, Pallas kernels, body(): pl.pallas_call(functools.partial(kernel, sizes), out_shape=(pltpu.VMEM((8...  51.8 us
    pallas_call x1, Pallas kernels, body(): pl.pallas_call(finish, out_shape=(jax.ShapeDtypeStruct((8, 8), f32), jax....  1.16 us

profile of v6, /device:TPU:1, one launch (start us, length us, event | category | flops | bytes accessed | tf_op | source)
XLA Modules:
  0.0 53.6 jit_solution(15058036976461587734)
XLA Ops:
  0.6 51.8 %shard_map.76 = (f32[8,8]{1,0:T(8,128)S(1)}, f32[16,3,8,128]{3,2,1,0:T(8,128)S(1)}, f32[128,128]{1,0:T(8,128)S(1)}, f32[384,128]{1,0:T(8,128)S(1)}) custom-call(bf16[8,256,128]{2,1,0:T(8,128)(2,1)} %q_hbm.1, bf16[1,256,128]{2,1,0:T(8,128)(2,1)} %k_hbm.1, s32[8,8]{1,0:T(8,128)} %samples_hbm.1, f32[128,128]{1,0:T(8,128)} %wq_hbm.1, f32[384,128]{1,0:T(8,128)} %wk_hbm.1), custom_call_target="tpu_custom_call" | custom-call | tf_op jit(solution)/shard_map/pallas_call | solution.py:410
  52.5 1.2 %shard_map.77 = (f32[8,8]{1,0:T(8,128)}, f32[128,128]{1,0:T(8,128)}, f32[384,128]{1,0:T(8,128)}) custom-call(f32[8,8]{1,0:T(8,128)S(1)} %get-tuple-element.7.loss_ref, f32[16,3,8,128]{3,2,1,0:T(8,128)S(1)} %get-tuple-element.8.total_ref, f32[128,128]{1,0:T(8,128)S(1)} %get-tuple-element.9.wq_ref, f32[384,128]{1,0:T(8,128)S(1)} %get-tuple-element.10.wk_ref), custom_call_target="tpu_custom_call" | custom-call | tf_op jit(solution)/shard_map/pallas_call | solution.py:442

commit v7 on v6

--- a/solution.py
+++ b/solution.py
@@ -56,6 +56,8 @@
     samples_ref,
     pooled,
     queries,
+    for_other,
+    tile_for_other,
     packed,
     returned,
     part,
@@ -64,6 +66,10 @@
     from_z,
     z_sum,
     load_sem,
+    for_other_recv,
+    tile_for_other_recv,
+    passed_send,
+    tile_passed_send,
     query_send,
     query_recv,
     pool_send,
@@ -125,6 +131,7 @@
     )
     touched = sorted({*near_z, *map(abs, upper), *map(abs, lower)}, reverse=True)
     near = [along_z(sign * d) for d in touched for sign in (1, -1)]
+    near += [{**target, "c": 1 - c} for target in near]
     near += [along_xy(n) for n in others]
     loads = [
         pltpu.make_async_copy(src, dst, load_sem.at[n])
@@ -207,10 +214,32 @@
             along_z(step),
         )
 
-    for d in reversed(near_z):
+    @pl.when(c == 0)
+    def start_core_0():
+        for n, sign in enumerate((1, -1)):
+            far_chip = {**along_z(sign * far), "c": 1}
+            send(queries.at[0], for_other.at[n], query_send, for_other_recv.at[n], far_chip)
+        for n, sign in enumerate((1, -1)):
+            far_chip = {**along_z(sign * far), "c": 1}
+            send(
+                pooled.at[0, 0, :6],
+                tile_for_other.at[n, :6],
+                pool_send,
+                tile_for_other_recv.at[n],
+                far_chip,
+            )
+
+    @pl.when(c == 1)
+    def start_core_1():
+        for sign in (1, -1):
+            pass_query(0, sign * far)
+        for sign in (1, -1):
+            pass_pool(0, sign * far)
+
+    for d in reversed(near_z[:-1]):
         for sign in (1, -1):
             pass_query(0, sign * d)
-    for d in reversed(near_z):
+    for d in reversed(near_z[:-1]):
         for sign in (1, -1):
             pass_pool(0, sign * d)
     for i in (2, 3, 1):
@@ -226,14 +255,36 @@
     places = jnp.sum(jnp.where(eye, column, 0.0), axis=0, keepdims=True).astype(jnp.int32)
     places = jnp.where(lanes < 64, places, 2 * BLOCK - 1)
 
-    for pass_on, kept, recv in (
-        (pass_query, queries, query_recv),
-        (pass_pool, pooled.at[0], pool_recv),
-    ):
-        for held, steps in zip(far_places, (upper, lower)):
-            wait_for(kept.at[held] if kept is queries else kept.at[held, :6], recv.at[group_of[held]])
+    @pl.when(c == 1)
+    def relay():
+        for n, (held, steps) in enumerate(zip(far_places, (upper, lower))):
+            wait_for(queries.at[held], query_recv.at[group_of[held]])
             for step in steps:
-                pass_on(held, step)
+                pass_query(held, step)
+            wait_for(for_other.at[n], for_other_recv.at[n])
+            for step in (*steps, 0):
+                at = (held + step) % nz
+                send(
+                    for_other.at[n],
+                    queries.at[at],
+                    passed_send,
+                    query_recv.at[group_of[at]],
+                    {**along_z(step), "c": 0},
+                )
+        for n, (held, steps) in enumerate(zip(far_places, (upper, lower))):
+            wait_for(pooled.at[0, held, :6], pool_recv.at[group_of[held]])
+            for step in steps:
+                pass_pool(held, step)
+            wait_for(tile_for_other.at[n, :6], tile_for_other_recv.at[n])
+            for step in (*steps, 0):
+                at = (held + step) % nz
+                send(
+                    tile_for_other.at[n, :6],
+                    pooled.at[0, at, :6],
+                    tile_passed_send,
+                    pool_recv.at[group_of[at]],
+                    {**along_z(step), "c": 0},
+                )
 
     wait_for(keys.at[1:4], keys_recv)
     exponent = math.log2(math.e) / math.sqrt(BLOCK)
@@ -266,7 +317,18 @@
                 back = nz - at
                 send(packed.at[at], returned.at[back], back_send, back_recv, along_z(-at))
 
+    def await_far(group, kind):
+        @pl.when(c == 0)
+        def core_0():
+            for held in far_places:
+                if held in group:
+                    if kind == "query":
+                        wait_for(queries.at[held], query_recv.at[group_of[held]])
+                    else:
+                        wait_for(pooled.at[0, held, :6], pool_recv.at[group_of[held]])
+
     def share_tiles(group, waited):
+        await_far(group, "pool")
         wait_for(pooled.at[0, : len(waited), :6], pool_recv.at[group_of[waited[0]]])
         for at in group:
             for i in (2, 3, 1):
@@ -275,6 +337,7 @@
                 )
 
     for n, (group, waited) in enumerate(zip(groups, waits)):
+        await_far(group, "query")
         score(group, waited)
         if n < len(groups) - 2:
             share_tiles(group, waited)
@@ -367,19 +430,24 @@
             send(z_sum, total_ref.at[place_of(0)], all_send, all_recv, along_xy(n))
         total_ref[place_of(0)] = total
 
-    wait_for(queries.at[1:], query_send)
-    wait_for(pooled.at[0, 1:, :6], pool_send)
+    passed = 2 + len(upper) + len(lower)
     wait_for(keys.at[1:], keys_send)
     wait_for(packed.at[1:], back_send)
     wait_for(pooled.at[1:, :, :6], tile_send)
 
     @pl.when(c == 0)
     def end_core_0():
+        wait_for(queries.at[: 2 * len(near_z)], query_send)
+        wait_for(pooled.at[0, : 2 * len(near_z), :6], pool_send)
         wait_for(part, sum_send)
         wait_for(part, all_recv)
 
     @pl.when(c == 1)
     def end_core_1():
+        wait_for(queries.at[1:], query_send)
+        wait_for(pooled.at[0, 1:, :6], pool_send)
+        wait_for(queries.at[:passed], passed_send)
+        wait_for(pooled.at[0, :passed, :6], tile_passed_send)
         wait_for(part.at[1:], sum_send)
         wait_for(from_z.at[1:], z_send)
         wait_for(from_slice.at[1:], all_send)
@@ -423,6 +491,8 @@
             pltpu.VMEM((8, 8), jnp.int32),
             pltpu.VMEM((4, nz, 8, BLOCK), f32),
             pltpu.VMEM((nz, 64, BLOCK), bf16),
+            pltpu.VMEM((2, 64, BLOCK), bf16),
+            pltpu.VMEM((2, 8, BLOCK), f32),
             pltpu.VMEM((nz, 8, BLOCK), f32),
             pltpu.VMEM((nz, 8, BLOCK), f32),
             pltpu.VMEM((chunks, *tile), f32),
@@ -431,6 +501,10 @@
             pltpu.VMEM((nz, *tile), f32),
             pltpu.VMEM(tile, f32),
             dma((5,)),
+            dma((2,)),
+            dma((2,)),
+            dma,
+            dma,
             dma,
             dma((len(ROUTES[nz][3]) + 2,)),
             dma,

time: 53.8 us -> 53.8 us (level)
  no operation moved by 1% of the time
where the time goes in v7:
time: 53.8 us; the launch traced here: 53.6 us
  Pallas kernels  53 us (99%)
  between operations  0.64 us (1%)
    pallas_call x1, Pallas kernels, body(): pl.pallas_call(functools.partial(kernel, sizes), out_shape=(pltpu.VMEM((8...  51.8 us
    pallas_call x1, Pallas kernels, body(): pl.pallas_call(finish, out_shape=(jax.ShapeDtypeStruct((8, 8), f32), jax....  1.16 us

profile of v7, /device:TPU:1, one launch (start us, length us, event | category | flops | bytes accessed | tf_op | source)
XLA Modules:
  0.0 53.6 jit_solution(11220809575434342112)
XLA Ops:
  0.6 51.8 %shard_map.76 = (f32[8,8]{1,0:T(8,128)S(1)}, f32[16,3,8,128]{3,2,1,0:T(8,128)S(1)}, f32[128,128]{1,0:T(8,128)S(1)}, f32[384,128]{1,0:T(8,128)S(1)}) custom-call(bf16[8,256,128]{2,1,0:T(8,128)(2,1)} %q_hbm.1, bf16[1,256,128]{2,1,0:T(8,128)(2,1)} %k_hbm.1, s32[8,8]{1,0:T(8,128)} %samples_hbm.1, f32[128,128]{1,0:T(8,128)} %wq_hbm.1, f32[384,128]{1,0:T(8,128)} %wk_hbm.1), custom_call_target="tpu_custom_call" | custom-call | tf_op jit(solution)/shard_map/pallas_call | solution.py:478
  52.5 1.2 %shard_map.77 = (f32[8,8]{1,0:T(8,128)}, f32[128,128]{1,0:T(8,128)}, f32[384,128]{1,0:T(8,128)}) custom-call(f32[8,8]{1,0:T(8,128)S(1)} %get-tuple-element.7.loss_ref, f32[16,3,8,128]{3,2,1,0:T(8,128)S(1)} %get-tuple-element.8.total_ref, f32[128,128]{1,0:T(8,128)S(1)} %get-tuple-element.9.wq_ref, f32[384,128]{1,0:T(8,128)S(1)} %get-tuple-element.10.wk_ref), custom_call_target="tpu_custom_call" | custom-call | tf_op jit(solution)/shard_map/pallas_call | solution.py:516

commit v8 on v6

--- a/solution.py
+++ b/solution.py
@@ -276,9 +276,9 @@
 
     for n, (group, waited) in enumerate(zip(groups, waits)):
         score(group, waited)
-        if n < len(groups) - 2:
+        if n < 1:
             share_tiles(group, waited)
-    for group, waited in list(zip(groups, waits))[-2:]:
+    for group, waited in list(zip(groups, waits))[1:]:
         share_tiles(group, waited)
     returned[0] = packed[0]
     loads[4].wait()

time: 53.8 us -> 53.8 us (level)
  no operation moved by 1% of the time
where the time goes in v8:
time: 53.8 us; the launch traced here: 53.6 us
  Pallas kernels  53 us (99%)
  between operations  0.64 us (1%)
    pallas_call x1, Pallas kernels, body(): pl.pallas_call(functools.partial(kernel, sizes), out_shape=(pltpu.VMEM((8...  51.8 us
    pallas_call x1, Pallas kernels, body(): pl.pallas_call(finish, out_shape=(jax.ShapeDtypeStruct((8, 8), f32), jax....  1.16 us

profile of v8, /device:TPU:1, one launch (start us, length us, event | category | flops | bytes accessed | tf_op | source)
XLA Modules:
  0.0 53.6 jit_solution(8747303372368813406)
XLA Ops:
  0.6 51.8 %shard_map.76 = (f32[8,8]{1,0:T(8,128)S(1)}, f32[16,3,8,128]{3,2,1,0:T(8,128)S(1)}, f32[128,128]{1,0:T(8,128)S(1)}, f32[384,128]{1,0:T(8,128)S(1)}) custom-call(bf16[8,256,128]{2,1,0:T(8,128)(2,1)} %q_hbm.1, bf16[1,256,128]{2,1,0:T(8,128)(2,1)} %k_hbm.1, s32[8,8]{1,0:T(8,128)} %samples_hbm.1, f32[128,128]{1,0:T(8,128)} %wq_hbm.1, f32[384,128]{1,0:T(8,128)} %wk_hbm.1), custom_call_target="tpu_custom_call" | custom-call | tf_op jit(solution)/shard_map/pallas_call | solution.py:410
  52.5 1.2 %shard_map.77 = (f32[8,8]{1,0:T(8,128)}, f32[128,128]{1,0:T(8,128)}, f32[384,128]{1,0:T(8,128)}) custom-call(f32[8,8]{1,0:T(8,128)S(1)} %get-tuple-element.7.loss_ref, f32[16,3,8,128]{3,2,1,0:T(8,128)S(1)} %get-tuple-element.8.total_ref, f32[128,128]{1,0:T(8,128)S(1)} %get-tuple-element.9.wq_ref, f32[384,128]{1,0:T(8,128)S(1)} %get-tuple-element.10.wk_ref), custom_call_target="tpu_custom_call" | custom-call | tf_op jit(solution)/shard_map/pallas_call | solution.py:442

commit v9 on v8

--- a/solution.py
+++ b/solution.py
@@ -23,7 +23,7 @@
         (1, 2, 4),
         (4, 3, 2, 1, -1),
         (-3, -2, -1, 1),
-        ((0, 1, 2, 15), (14, 4, 12, 5), (6, 7, 8, 9), (10, 11, 3, 13)),
+        ((0, 1, 2, 15), (14, 4), (12, 3, 13, 5), (6, 7, 8, 9), (10, 11)),
     ),
 }
 
@@ -256,7 +256,7 @@
                 sums.append(jnp.sum(weights, axis=0, keepdims=True))
         tops = jnp.concatenate(tops, axis=0)
         sums = jnp.concatenate(sums, axis=0)
-        for pair in range(2):
+        for pair in range(len(slots) // 2):
             top = tops[:, pair * BLOCK : (pair + 1) * BLOCK]
             mass = sums[:, pair * BLOCK : (pair + 1) * BLOCK]
             packed[slots[2 * pair]] = jnp.where(first, top, pltpu.roll(mass, 64, 1))

time: 53.8 us -> 53.8 us (level)
  no operation moved by 1% of the time
where the time goes in v9:
time: 53.8 us; the launch traced here: 53.6 us
  Pallas kernels  53 us (99%)
  between operations  0.64 us (1%)
    pallas_call x1, Pallas kernels, body(): pl.pallas_call(functools.partial(kernel, sizes), out_shape=(pltpu.VMEM((8...  51.8 us
    pallas_call x1, Pallas kernels, body(): pl.pallas_call(finish, out_shape=(jax.ShapeDtypeStruct((8, 8), f32), jax....  1.16 us

profile of v9, /device:TPU:1, one launch (start us, length us, event | category | flops | bytes accessed | tf_op | source)
XLA Modules:
  0.0 53.6 jit_solution(8950709060379614688)
XLA Ops:
  0.6 51.8 %shard_map.76 = (f32[8,8]{1,0:T(8,128)S(1)}, f32[16,3,8,128]{3,2,1,0:T(8,128)S(1)}, f32[128,128]{1,0:T(8,128)S(1)}, f32[384,128]{1,0:T(8,128)S(1)}) custom-call(bf16[8,256,128]{2,1,0:T(8,128)(2,1)} %q_hbm.1, bf16[1,256,128]{2,1,0:T(8,128)(2,1)} %k_hbm.1, s32[8,8]{1,0:T(8,128)} %samples_hbm.1, f32[128,128]{1,0:T(8,128)} %wq_hbm.1, f32[384,128]{1,0:T(8,128)} %wk_hbm.1), custom_call_target="tpu_custom_call" | custom-call | tf_op jit(solution)/shard_map/pallas_call | solution.py:410
  52.5 1.2 %shard_map.77 = (f32[8,8]{1,0:T(8,128)}, f32[128,128]{1,0:T(8,128)}, f32[384,128]{1,0:T(8,128)}) custom-call(f32[8,8]{1,0:T(8,128)S(1)} %get-tuple-element.7.loss_ref, f32[16,3,8,128]{3,2,1,0:T(8,128)S(1)} %get-tuple-element.8.total_ref, f32[128,128]{1,0:T(8,128)S(1)} %get-tuple-element.9.wq_ref, f32[384,128]{1,0:T(8,128)S(1)} %get-tuple-element.10.wk_ref), custom_call_target="tpu_custom_call" | custom-call | tf_op jit(solution)/shard_map/pallas_call | solution.py:442

commit v10 on v8

--- a/solution.py
+++ b/solution.py
@@ -23,7 +23,7 @@
         (1, 2, 4),
         (4, 3, 2, 1, -1),
         (-3, -2, -1, 1),
-        ((0, 1, 2, 15), (14, 4, 12, 5), (6, 7, 8, 9), (10, 11, 3, 13)),
+        ((0, 1, 2, 15), (14, 4, 12, 13), (8, 7, 9, 6), (10, 11, 3, 5)),
     ),
 }
 

time: 53.8 us -> 53.7 us (level)
  no operation moved by 1% of the time
where the time goes in v10:
time: 53.7 us; the launch traced here: 53.6 us
  Pallas kernels  52.9 us (99%)
  between operations  0.64 us (1%)
    pallas_call x1, Pallas kernels, body(): pl.pallas_call(functools.partial(kernel, sizes), out_shape=(pltpu.VMEM((8...  51.8 us
    pallas_call x1, Pallas kernels, body(): pl.pallas_call(finish, out_shape=(jax.ShapeDtypeStruct((8, 8), f32), jax....  1.16 us

profile of v10, /device:TPU:1, one launch (start us, length us, event | category | flops | bytes accessed | tf_op | source)
XLA Modules:
  0.0 53.6 jit_solution(14954744666570105900)
XLA Ops:
  0.6 51.8 %shard_map.76 = (f32[8,8]{1,0:T(8,128)S(1)}, f32[16,3,8,128]{3,2,1,0:T(8,128)S(1)}, f32[128,128]{1,0:T(8,128)S(1)}, f32[384,128]{1,0:T(8,128)S(1)}) custom-call(bf16[8,256,128]{2,1,0:T(8,128)(2,1)} %q_hbm.1, bf16[1,256,128]{2,1,0:T(8,128)(2,1)} %k_hbm.1, s32[8,8]{1,0:T(8,128)} %samples_hbm.1, f32[128,128]{1,0:T(8,128)} %wq_hbm.1, f32[384,128]{1,0:T(8,128)} %wk_hbm.1), custom_call_target="tpu_custom_call" | custom-call | tf_op jit(solution)/shard_map/pallas_call | solution.py:410
  52.4 1.2 %shard_map.77 = (f32[8,8]{1,0:T(8,128)}, f32[128,128]{1,0:T(8,128)}, f32[384,128]{1,0:T(8,128)}) custom-call(f32[8,8]{1,0:T(8,128)S(1)} %get-tuple-element.7.loss_ref, f32[16,3,8,128]{3,2,1,0:T(8,128)S(1)} %get-tuple-element.8.total_ref, f32[128,128]{1,0:T(8,128)S(1)} %get-tuple-element.9.wq_ref, f32[384,128]{1,0:T(8,128)S(1)} %get-tuple-element.10.wk_ref), custom_call_target="tpu_custom_call" | custom-call | tf_op jit(solution)/shard_map/pallas_call | solution.py:442
